TPU v7x, 32 devices: a whole 2x2x4 slice. The times are simulated.
32 devices in a mesh: rep: 2 (over x), ctx: 8 (over z, y), tp: 2 (over core).
Axes of the slice: x: 2, y: 2, z: 4, core: 2. Of those that a mesh axis runs over, the one named last changes fastest.
Arguments:
- queries: bfloat16 [4096, 4096], P(('rep', 'ctx'), 'tp'), parts along dimension 0, may hold values from -8 to 8
- rotated_key_rows: bfloat16 [4096, 512], P(('rep', 'ctx'), 'tp'), parts along dimension 0, may hold values from -8 to 8
- ordered_value_rows: bfloat16 [4096, 512], P(('rep', 'ctx'), 'tp'), parts along dimension 0, may hold values from -6 to 6
- block_order: int32 [32], P('rep'), parts along dimension 0, may hold values from 0 to 15, each once
- live_blocks: int32 [32, 12], P('rep'), parts along dimension 0, may hold values from -1 to 15, as said below
Outputs:
- attended: bfloat16 [4096, 4096], P(('rep', 'ctx', 'tp')), parts along dimension 0
- log_norm: float32 [64, 2048], P(('rep', 'tp'), 'ctx'), parts along dimension 0
There are 2 independent parts, one for each index of `rep`. A program takes and returns all parts, laid end to end along the dimension named above; each array names one. Nothing has to cross between parts.
Inputs may be any that keep to these rules, and one draw needn't show every extreme that they name: `live_blocks`: row s names block s in its first slot, then distinct blocks before s, then -1 in every unused slot; row 15 fills all 12 slots.
All inputs are finite; a program needn't handle non-finite values.
Results may differ from a plain program's by a relative error of at most 0.008.
Values may be sent and summed in bfloat16 or wider, within the bound.
A program may use at most 128 MiB of HBM per device.

v0:
```python
import functools
import math

import jax
import jax.numpy as jnp
from jax import lax
from jax.experimental import pallas as pl
from jax.experimental.pallas import tpu as pltpu
from jax.sharding import PartitionSpec as P

HEAD_SIZE = 128
BLOCK_TOKENS = 128
CHUNK = 256
STRIP = 16
SLOTS = 4
FAR = 1e30
HUGE = 3e38
MESH = pl.DeviceIdType.MESH


def grid_of(count):
    minor = max(d for d in range(1, math.isqrt(count) + 1) if count % d == 0)
    return count // minor, minor


def kernel(
    dims,
    queries,
    keys,
    values,
    block_order,
    live_blocks,
    attended,
    log_norm,
    held,
    raw_queries,
    turned_queries,
    total,
    peak,
    weight_sum,
    leaving,
    limits,
    scores,
    load_sem,
    send_sem,
    recv_sem,
    swap_send,
    swap_recv,
):
    major, minor, tp_size, kv_local, groups, blocks_here, slots_live = dims
    factor = HEAD_SIZE ** (-0.5)
    scale = factor * math.log2(math.e)
    width = groups * BLOCK_TOKENS
    rows = blocks_here * BLOCK_TOKENS
    me = lax.axis_index("ctx")
    mine = lax.axis_index("tp")
    a, b = me // minor, me % minor

    loads = [
        pltpu.make_async_copy(keys, held.at[me, 0], load_sem.at[0]),
        pltpu.make_async_copy(values, held.at[me, 1], load_sem.at[1]),
        pltpu.make_async_copy(queries, raw_queries, load_sem.at[2]),
    ]
    for load in loads:
        load.start()

    barrier = pltpu.get_barrier_semaphore()
    sides = (
        (a > 0, me - minor),
        (a < major - 1, me + minor),
        (b > 0, me - 1),
        (b < minor - 1, me + 1),
    )
    for there, who in sides:

        @pl.when(there)
        def _(who=who):
            pl.semaphore_signal(barrier, inc=1, device_id={"ctx": who}, device_id_type=MESH)

    for turn in range(1, tp_size):
        peer = (mine + turn) % tp_size
        pl.semaphore_signal(barrier, inc=1, device_id={"tp": peer}, device_id_type=MESH)
    expected = jnp.int32(tp_size - 1)
    for there, _ in sides:
        expected = expected + there.astype(jnp.int32)
    pl.semaphore_wait(barrier, expected)

    def onward(slot, piece, i, j):
        wanted = (
            (j == b) & (i >= a) & (a > 0),
            (j == b) & (i <= a) & (a < major - 1),
            (j >= b) & (b > 0),
            (j <= b) & (b < minor - 1),
        )
        for side in range(4):
            copy = pltpu.make_async_remote_copy(
                src_ref=held.at[slot, piece],
                dst_ref=held.at[slot, piece],
                send_sem=send_sem.at[slot, piece, side],
                recv_sem=recv_sem.at[slot, piece],
                device_id={"ctx": sides[side][1]},
                device_id_type=MESH,
            )
            yield wanted[side], copy

    def send_on(slot, piece, i, j):
        for wanted, copy in onward(slot, piece, i, j):

            @pl.when(wanted)
            def _(copy=copy):
                copy.start()

    def find_limits(slot):
        for query_block in range(blocks_here):
            my_seq = block_order[0, me * blocks_here + query_block]
            found = [jnp.bool_(False)] * blocks_here
            names = [block_order[0, slot * blocks_here + kb] for kb in range(blocks_here)]
            for entry in range(slots_live):
                listed = live_blocks[my_seq, entry]
                found = [f | (listed == name) for f, name in zip(found, names)]
            for kb in range(blocks_here):
                limits[0, query_block * blocks_here + kb] = jnp.where(found[kb], HUGE, -FAR)
                limits[1, query_block * blocks_here + kb] = jnp.where(found[kb], -HUGE, FAR)

    def attend(slot, own):
        find_limits(slot)
        keys_here = blocks_here * BLOCK_TOKENS
        units = [
            (query_block, h, start)
            for h in range(kv_local)
            for query_block in range(blocks_here)
            for start in range(0, width, CHUNK)
        ]
        turned_values = [
            jnp.transpose(held[slot, 1, :, pl.ds(h * HEAD_SIZE, HEAD_SIZE)])
            for h in range(kv_local)
        ]

        def score(u):
            query_block, h, start = units[u]
            part = jnp.dot(
                held[slot, 0, :, pl.ds(h * HEAD_SIZE, HEAD_SIZE)],
                turned_queries[query_block, h, :, pl.ds(start, CHUNK)],
                preferred_element_type=jnp.float32,
            )
            tops = []
            for kb in range(blocks_here):
                block = part[kb * BLOCK_TOKENS : (kb + 1) * BLOCK_TOKENS]
                if own and kb == query_block:
                    key_at = lax.broadcasted_iota(jnp.int32, block.shape, 0)
                    row_at = lax.broadcasted_iota(jnp.int32, block.shape, 1) % BLOCK_TOKENS
                    block = jnp.where(key_at <= row_at, block, -FAR)
                scores[u % SLOTS, pl.ds(kb * BLOCK_TOKENS, BLOCK_TOKENS), :] = block
                tops.append(jnp.max(block, axis=0, keepdims=True))
            return tops

        def absorb(u, tops):
            query_block, h, start = units[u]
            lanes = pl.ds(start, CHUNK)
            first = query_block * blocks_here
            new_peak = None
            for kb, top in enumerate(tops):
                top = jnp.minimum(top, limits[0, first + kb])
                new_peak = top if new_peak is None else jnp.maximum(new_peak, top)
            if not own:
                old_peak = peak[query_block, h, :, lanes]
                new_peak = jnp.maximum(new_peak, old_peak)
            peak[query_block, h, :, lanes] = new_peak
            level = new_peak * scale
            added = None
            low = []
            for kb in range(blocks_here):
                floor = jnp.maximum(level, limits[1, first + kb])
                for at in range(kb * BLOCK_TOKENS, (kb + 1) * BLOCK_TOKENS, STRIP):
                    w = jnp.exp2(scores[u % SLOTS, pl.ds(at, STRIP), :] * scale - floor)
                    added = w if added is None else added + w
                    low.append(w.astype(jnp.bfloat16))
            added = jnp.sum(added, axis=0, keepdims=True)
            product = jnp.dot(
                turned_values[h],
                jnp.concatenate(low, axis=0),
                preferred_element_type=jnp.float32,
            )
            if own:
                weight_sum[query_block, h, :, lanes] = added
                total[query_block, h, :, lanes] = product
            else:
                fade = jnp.exp2((old_peak - new_peak) * scale)
                weight_sum[query_block, h, :, lanes] = (
                    weight_sum[query_block, h, :, lanes] * fade + added
                )
                total[query_block, h, :, lanes] = total[query_block, h, :, lanes] * fade + product

        waiting = [score(u) for u in range(SLOTS - 1)]
        for u in range(len(units)):
            if u + SLOTS - 1 < len(units):
                waiting.append(score(u + SLOTS - 1))
            absorb(u, waiting[u])

    for piece in range(2):
        loads[piece].wait()
        send_on(me, piece, a, b)
    loads[2].wait()

    def turn_block(query_block, carry):
        at = pl.ds(pl.multiple_of(query_block * BLOCK_TOKENS, BLOCK_TOKENS), BLOCK_TOKENS)
        for h in range(kv_local):
            for g in range(groups):
                head = h * groups + g
                turned_queries[query_block, h, :, pl.ds(g * BLOCK_TOKENS, BLOCK_TOKENS)] = (
                    jnp.transpose(raw_queries[at, pl.ds(head * HEAD_SIZE, HEAD_SIZE)])
                )
        return carry

    lax.fori_loop(0, blocks_here, turn_block, 0)
    attend(me, True)

    rounds = (major + minor - 1) * minor * 4

    def place_of(turn):
        far, near = turn // (4 * minor), (turn // 4) % minor
        up, along = (turn // 2) % 2, turn % 2
        reach = far - near
        i = a + reach * (1 - 2 * up)
        j = b + near * (1 - 2 * along)
        fits = (reach >= 0) & (i >= 0) & (i < major) & (j >= 0) & (j < minor)
        fits = fits & ((reach > 0) | (up == 0)) & ((near > 0) | (along == 0))
        return fits, i, j

    def one_shard(turn, carry):
        fits, i, j = place_of(turn)

        @pl.when(fits & (far_from(i, j)))
        def _():
            slot = i * minor + j
            for piece in range(2):
                pltpu.make_async_copy(
                    held.at[slot, piece], held.at[slot, piece], recv_sem.at[slot, piece]
                ).wait()
                send_on(slot, piece, i, j)
            attend(slot, False)

        return carry

    def far_from(i, j):
        return (i != a) | (j != b)

    lax.fori_loop(1, rounds, one_shard, 0)

    per_peer = blocks_here // tp_size
    wide = kv_local * width

    def finish(query_block, h, put):
        at = pl.ds(pl.multiple_of(query_block * BLOCK_TOKENS, BLOCK_TOKENS), BLOCK_TOKENS)
        for g in range(groups):
            lanes = pl.ds(g * BLOCK_TOKENS, BLOCK_TOKENS)
            bottom = weight_sum[query_block, h, :, lanes]
            normed = (total[query_block, h, :, lanes] * (1.0 / bottom)).astype(jnp.bfloat16)
            put(h * groups + g, jnp.transpose(normed))
            log_norm[pl.ds(h * groups + g, 1), at] = (
                peak[query_block, h, :, lanes] * factor + jnp.log(bottom)
            )

    swaps = []
    for turn in range(1, tp_size + 1):
        peer = (mine + turn) % tp_size
        for k in range(per_peer):
            query_block = peer * per_peer + k
            out_rows = pl.ds(k * BLOCK_TOKENS, BLOCK_TOKENS)
            for h in range(kv_local):
                if turn < tp_size:

                    def put(head, tile, query_block=query_block):
                        leaving[query_block, :, pl.ds(head * HEAD_SIZE, HEAD_SIZE)] = tile

                else:

                    def put(head, tile, out_rows=out_rows):
                        at = pl.multiple_of(mine * wide + head * HEAD_SIZE, HEAD_SIZE)
                        attended[out_rows, pl.ds(at, HEAD_SIZE)] = tile

                finish(query_block, h, put)
                if turn < tp_size:
                    source = pl.ds(h * width, width)
                    target = pl.ds(pl.multiple_of(mine * wide + h * width, HEAD_SIZE), width)
                    copy = pltpu.make_async_remote_copy(
                        src_ref=leaving.at[query_block, :, source],
                        dst_ref=attended.at[out_rows, target],
                        send_sem=swap_send.at[turn - 1, k, h],
                        recv_sem=swap_recv.at[turn - 1, k, h],
                        device_id={"tp": peer},
                        device_id_type=MESH,
                    )
                    copy.start()
                    swaps.append(copy)

    def settle(turn, carry):
        fits, i, j = place_of(turn)

        @pl.when(fits)
        def _():
            slot = i * minor + j
            for piece in range(2):
                for wanted, copy in onward(slot, piece, i, j):

                    @pl.when(wanted)
                    def _(copy=copy):
                        copy.wait_send()

        return carry

    lax.fori_loop(0, rounds, settle, 0)
    for copy in swaps:
        copy.wait()


def body(tp_size, ctx_size, queries, rotated_key_rows, ordered_value_rows, block_order, live_blocks):
    tok_rows, own_columns = queries.shape
    kv_columns = rotated_key_rows.shape[1]
    kv_local = kv_columns // HEAD_SIZE
    heads_local = own_columns // HEAD_SIZE
    groups = heads_local // kv_local
    blocks_here = tok_rows // BLOCK_TOKENS
    width = groups * BLOCK_TOKENS
    major, minor = grid_of(ctx_size)
    dims = (major, minor, tp_size, kv_local, groups, blocks_here, live_blocks.shape[1])
    per_peer = blocks_here // tp_size
    whole = pl.BlockSpec(memory_space=pltpu.VMEM)
    small = pl.BlockSpec(memory_space=pltpu.SMEM)
    apart = pl.BlockSpec(memory_space=pl.ANY)
    results = pl.pallas_call(
        functools.partial(kernel, dims),
        out_shape=(
            pltpu.VMEM((tok_rows // tp_size, own_columns * tp_size), jnp.bfloat16),
            pltpu.VMEM((heads_local, tok_rows), jnp.float32),
        ),
        in_specs=[apart, apart, apart, small, small],
        out_specs=(whole, whole),
        scratch_shapes=[
            pltpu.VMEM((ctx_size, 2, tok_rows, kv_columns), jnp.bfloat16),
            pltpu.VMEM((tok_rows, own_columns), jnp.bfloat16),
            pltpu.VMEM((blocks_here, kv_local, HEAD_SIZE, width), jnp.bfloat16),
            pltpu.VMEM((blocks_here, kv_local, HEAD_SIZE, width), jnp.float32),
            pltpu.VMEM((blocks_here, kv_local, 1, width), jnp.float32),
            pltpu.VMEM((blocks_here, kv_local, 1, width), jnp.float32),
            pltpu.VMEM((blocks_here, BLOCK_TOKENS, own_columns), jnp.bfloat16),
            pltpu.SMEM((2, blocks_here * blocks_here), jnp.float32),
            pltpu.VMEM((SLOTS, tok_rows, CHUNK), jnp.float32),
            pltpu.SemaphoreType.DMA((3,)),
            pltpu.SemaphoreType.DMA((ctx_size, 2, 4)),
            pltpu.SemaphoreType.DMA((ctx_size, 2)),
            pltpu.SemaphoreType.DMA((tp_size - 1, per_peer, kv_local)),
            pltpu.SemaphoreType.DMA((tp_size - 1, per_peer, kv_local)),
        ],
        compiler_params=pltpu.CompilerParams(collective_id=0, has_side_effects=True),
        name="gather_attend",
    )(queries, rotated_key_rows, ordered_value_rows, block_order.reshape(1, -1), live_blocks)
    return results


def solution(mesh):
    placed = (
        P(("rep", "ctx"), "tp"),
        P(("rep", "ctx"), "tp"),
        P(("rep", "ctx"), "tp"),
        P("rep"),
        P("rep", None),
    )
    return jax.shard_map(
        functools.partial(body, mesh.shape["tp"], mesh.shape["ctx"]),
        mesh=mesh,
        in_specs=placed,
        out_specs=(P(("rep", "ctx", "tp"), None), P(("rep", "tp"), "ctx")),
        check_vma=False,
    )
```

profile of v0, /device:TPU:26, one launch (start us, length us, event | category | flops | bytes accessed | tf_op | source)
XLA Modules:
  0.0 36.1 jit_solution(2187846530234544280)
XLA Ops:
  0.6 33.9 %gather_attend.1 = (bf16[128,4096]{1,0:T(8,128)(2,1)S(1)}, f32[16,256]{1,0:T(8,128)S(1)}) custom-call(bf16[256,2048]{1,0:T(8,128)(2,1)} %queries.1, bf16[256,256]{1,0:T(8,128)(2,1)} %keys.1, bf16[256,256]{1,0:T(8,128)(2,1)} %values.1, s32[1,16]{1,0:T(1,128)} %bitcast.1, s32[16,12]{1,0:T(8,128)} %live_blocks.1), custom_call_target="tpu_custom_call" | custom-call | tf_op jit(solution)/shard_map/gather_attend/pallas_call | solution.py:331
  34.6 1.0 %copy.9 = bf16[128,4096]{1,0:T(8,128)(2,1)} copy(bf16[128,4096]{1,0:T(8,128)(2,1)S(1)} %get-tuple-element.2) | data formatting | bytes 2097152
  35.5 0.6 %copy.10 = f32[16,256]{1,0:T(8,128)} copy(f32[16,256]{1,0:T(8,128)S(1)} %get-tuple-element.3) | data formatting | bytes 32768
where the time goes:
time: 36.4 us; the launch traced here: 36.1 us
  Pallas kernels  33.9 us (93%)
  local copies, waits for them, and re-layouts  1.58 us (4%)
  between operations  0.64 us (2%)
    pallas_call x1, Pallas kernels, body(): pl.pallas_call(functools.partial(kernel, dims), out_shape=(pltpu.VMEM((to...  33.9 us
    unnamed x2, local copies, waits for them, and re-layouts  1.58 us

commit v1 on v0

v1 whole, which is shorter than its diff:
```python
import functools
import math

import jax
import jax.numpy as jnp
from jax import lax
from jax.experimental import pallas as pl
from jax.experimental.pallas import tpu as pltpu
from jax.sharding import PartitionSpec as P

HEAD_SIZE = 128
BLOCK_TOKENS = 128
CHUNK = 256
STRIP = 16
SLOTS = 4
FAR = 1e30
HUGE = 3e38
MESH = pl.DeviceIdType.MESH


def grid_of(count):
    minor = max(d for d in range(1, math.isqrt(count) + 1) if count % d == 0)
    return count // minor, minor


def kernel(
    dims,
    queries,
    keys,
    values,
    block_order,
    live_blocks,
    attended,
    log_norm,
    held,
    raw_queries,
    turned_queries,
    total,
    peak,
    weight_sum,
    leaving,
    limits,
    scores,
    load_sem,
    send_sem,
    recv_sem,
    swap_send,
    swap_recv,
):
    major, minor, tp_size, kv_local, groups, blocks_here, parts, slots_live = dims
    factor = HEAD_SIZE ** (-0.5)
    scale = factor * math.log2(math.e)
    width = groups * BLOCK_TOKENS
    per_part = blocks_here // parts
    me = lax.axis_index("ctx")
    mine = lax.axis_index("tp")
    a, b = me // minor, me % minor

    loads = {}
    for part in range(parts):
        for h in range(kv_local):
            for kb in range(per_part):
                at = pl.ds((part * per_part + kb) * BLOCK_TOKENS, BLOCK_TOKENS)
                lanes = pl.ds(h * HEAD_SIZE, HEAD_SIZE)
                for kind, source in enumerate((keys, values)):
                    loads[part, h, kb, kind] = pltpu.make_async_copy(
                        source.at[at, lanes],
                        held.at[me, part, h, kb, kind],
                        load_sem.at[part, h, kb, kind],
                    )
    for load in loads.values():
        load.start()
    load_queries = pltpu.make_async_copy(queries, raw_queries, load_sem.at[parts, 0, 0, 0])
    load_queries.start()

    barrier = pltpu.get_barrier_semaphore()
    sides = (
        (a > 0, me - minor),
        (a < major - 1, me + minor),
        (b > 0, me - 1),
        (b < minor - 1, me + 1),
    )
    for there, who in sides:

        @pl.when(there)
        def _(who=who):
            pl.semaphore_signal(barrier, inc=1, device_id={"ctx": who}, device_id_type=MESH)

    for turn in range(1, tp_size):
        peer = (mine + turn) % tp_size
        pl.semaphore_signal(barrier, inc=1, device_id={"tp": peer}, device_id_type=MESH)
    expected = jnp.int32(tp_size - 1)
    for there, _ in sides:
        expected = expected + there.astype(jnp.int32)
    pl.semaphore_wait(barrier, expected)

    def onward(part, i, j):
        column_first = j == b
        row_first = (i == 0) | (i == major - 1) if part == parts - 1 and parts > 1 else jnp.bool_(False)
        along = column_first | row_first
        across = (i == a) | jnp.logical_not(row_first)
        return (
            (i >= a) & (a > 0) & along,
            (i <= a) & (a < major - 1) & along,
            (j >= b) & (b > 0) & across,
            (j <= b) & (b < minor - 1) & across,
        )

    def send_on(slot, part, h, i, j):
        for side, wanted in enumerate(onward(part, i, j)):

            @pl.when(wanted)
            def _(side=side):
                pltpu.make_async_remote_copy(
                    src_ref=held.at[slot, part, h],
                    dst_ref=held.at[slot, part, h],
                    send_sem=send_sem.at[slot, part, side],
                    recv_sem=recv_sem.at[slot, part, h],
                    device_id={"ctx": sides[side][1]},
                    device_id_type=MESH,
                ).start()

    def settle(slot, i, j):
        for part in range(parts):
            for side, wanted in enumerate(onward(part, i, j)):

                @pl.when(wanted)
                def _(part=part, side=side):
                    pltpu.make_async_copy(
                        held.at[slot, part], held.at[slot, part], send_sem.at[slot, part, side]
                    ).wait()

    def find_limits(slot):
        for query_block in range(blocks_here):
            my_seq = block_order[0, me * blocks_here + query_block]
            found = [jnp.bool_(False)] * blocks_here
            names = [block_order[0, slot * blocks_here + kb] for kb in range(blocks_here)]
            for entry in range(slots_live):
                listed = live_blocks[my_seq, entry]
                found = [f | (listed == name) for f, name in zip(found, names)]
            for kb in range(blocks_here):
                limits[0, query_block * blocks_here + kb] = jnp.where(found[kb], HUGE, -FAR)
                limits[1, query_block * blocks_here + kb] = jnp.where(found[kb], -HUGE, FAR)

    def attend(slot, h, own):
        units = [
            (query_block, start)
            for query_block in range(blocks_here)
            for start in range(0, width, CHUNK)
        ]
        blocks = [(kb // per_part, kb % per_part) for kb in range(blocks_here)]
        keys_here = jnp.concatenate([held[slot, part, h, kb, 0] for part, kb in blocks], axis=0)
        turned_values = jnp.transpose(
            jnp.concatenate([held[slot, part, h, kb, 1] for part, kb in blocks], axis=0)
        )

        def score(u):
            query_block, start = units[u]
            part = jnp.dot(
                keys_here,
                turned_queries[query_block, h, :, pl.ds(start, CHUNK)],
                preferred_element_type=jnp.float32,
            )
            tops = []
            for kb in range(blocks_here):
                block = part[kb * BLOCK_TOKENS : (kb + 1) * BLOCK_TOKENS]
                if own and kb == query_block:
                    key_at = lax.broadcasted_iota(jnp.int32, block.shape, 0)
                    row_at = lax.broadcasted_iota(jnp.int32, block.shape, 1) % BLOCK_TOKENS
                    block = jnp.where(key_at <= row_at, block, -FAR)
                scores[u % SLOTS, pl.ds(kb * BLOCK_TOKENS, BLOCK_TOKENS), :] = block
                tops.append(jnp.max(block, axis=0, keepdims=True))
            return tops

        def absorb(u, tops):
            query_block, start = units[u]
            lanes = pl.ds(start, CHUNK)
            first = query_block * blocks_here
            new_peak = None
            for kb, top in enumerate(tops):
                top = jnp.minimum(top, limits[0, first + kb])
                new_peak = top if new_peak is None else jnp.maximum(new_peak, top)
            if not own:
                old_peak = peak[query_block, h, :, lanes]
                new_peak = jnp.maximum(new_peak, old_peak)
            peak[query_block, h, :, lanes] = new_peak
            level = new_peak * scale
            added = None
            low = []
            for kb in range(blocks_here):
                floor = jnp.maximum(level, limits[1, first + kb])
                for at in range(kb * BLOCK_TOKENS, (kb + 1) * BLOCK_TOKENS, STRIP):
                    w = jnp.exp2(scores[u % SLOTS, pl.ds(at, STRIP), :] * scale - floor)
                    added = w if added is None else added + w
                    low.append(w.astype(jnp.bfloat16))
            added = jnp.sum(added, axis=0, keepdims=True)
            product = jnp.dot(
                turned_values,
                jnp.concatenate(low, axis=0),
                preferred_element_type=jnp.float32,
            )
            if own:
                weight_sum[query_block, h, :, lanes] = added
                total[query_block, h, :, lanes] = product
            else:
                fade = jnp.exp2((old_peak - new_peak) * scale)
                weight_sum[query_block, h, :, lanes] = (
                    weight_sum[query_block, h, :, lanes] * fade + added
                )
                total[query_block, h, :, lanes] = total[query_block, h, :, lanes] * fade + product

        waiting = [score(u) for u in range(SLOTS - 1)]
        for u in range(len(units)):
            if u + SLOTS - 1 < len(units):
                waiting.append(score(u + SLOTS - 1))
            absorb(u, waiting[u])

    per_peer = blocks_here // tp_size
    wide = kv_local * width

    def swap(turn, k, h):
        peer = (mine + turn) % tp_size
        source = pl.ds(h * width, width)
        target = pl.ds(pl.multiple_of(mine * wide + h * width, HEAD_SIZE), width)
        return pltpu.make_async_remote_copy(
            src_ref=leaving.at[peer * per_peer + k, :, source],
            dst_ref=attended.at[pl.ds(k * BLOCK_TOKENS, BLOCK_TOKENS), target],
            send_sem=swap_send.at[turn - 1, k, h],
            recv_sem=swap_recv.at[turn - 1, k, h],
            device_id={"tp": peer},
            device_id_type=MESH,
        )

    def finish(h):
        for turn in range(1, tp_size + 1):
            peer = (mine + turn) % tp_size
            for k in range(per_peer):
                query_block = peer * per_peer + k
                at = pl.ds(pl.multiple_of(query_block * BLOCK_TOKENS, BLOCK_TOKENS), BLOCK_TOKENS)
                for g in range(groups):
                    head = h * groups + g
                    lanes = pl.ds(g * BLOCK_TOKENS, BLOCK_TOKENS)
                    bottom = weight_sum[query_block, h, :, lanes]
                    normed = total[query_block, h, :, lanes] * (1.0 / bottom)
                    tile = jnp.transpose(normed.astype(jnp.bfloat16))
                    if turn < tp_size:
                        leaving[query_block, :, pl.ds(head * HEAD_SIZE, HEAD_SIZE)] = tile
                    else:
                        to = pl.multiple_of(mine * wide + head * HEAD_SIZE, HEAD_SIZE)
                        attended[pl.ds(k * BLOCK_TOKENS, BLOCK_TOKENS), pl.ds(to, HEAD_SIZE)] = tile
                    log_norm[pl.ds(head, 1), at] = (
                        peak[query_block, h, :, lanes] * factor + jnp.log(bottom)
                    )
                if turn < tp_size:
                    swap(turn, k, h).start()

    for part in range(parts):
        for h in range(kv_local):
            for kb in range(per_part):
                for kind in range(2):
                    loads[part, h, kb, kind].wait()
    for h in range(kv_local):
        for part in range(parts):
            send_on(me, part, h, a, b)
    load_queries.wait()

    def turn_block(query_block, carry):
        at = pl.ds(pl.multiple_of(query_block * BLOCK_TOKENS, BLOCK_TOKENS), BLOCK_TOKENS)
        for h in range(kv_local):
            for g in range(groups):
                head = h * groups + g
                turned_queries[query_block, h, :, pl.ds(g * BLOCK_TOKENS, BLOCK_TOKENS)] = (
                    jnp.transpose(raw_queries[at, pl.ds(head * HEAD_SIZE, HEAD_SIZE)])
                )
        return carry

    lax.fori_loop(0, blocks_here, turn_block, 0)
    find_limits(me)
    for h in range(kv_local):
        attend(me, h, True)

    def nearest(x, n, k):
        both = jnp.minimum(x, n - 1 - x)
        away = 1 - 2 * (2 * x > n - 1).astype(jnp.int32)
        paired = ((k + 1) // 2) * (2 * (k % 2) - 1)
        return x + away * jnp.where(k <= 2 * both, paired, k - both)

    lag = 1 + ((a > 0) & (a < major - 1)).astype(jnp.int32)

    def place_of(turn):
        l = turn % minor
        k = turn // minor - lag * l
        fits = (k >= 0) & (k < major)
        return fits, k, l, nearest(a, major, k), nearest(b, minor, l)

    rounds = (major + 2 * (minor - 1)) * minor

    def one_shard(turn, carry):
        fits, k, l, i, j = place_of(turn)
        slot = i * minor + j
        last = (k == major - 1) & (l == minor - 1)

        @pl.when(fits & (k + l > 0))
        def _():
            @pl.when(last)
            def _():
                lax.fori_loop(0, rounds, settle_early, 0)

            find_limits(slot)
            for h in range(kv_local):
                for part in range(parts):
                    pltpu.make_async_copy(
                        held.at[slot, part, h], held.at[slot, part, h], recv_sem.at[slot, part, h]
                    ).wait()
                    send_on(slot, part, h, i, j)
                attend(slot, h, False)

                @pl.when(last)
                def _(h=h):
                    finish(h)

        return carry

    def settle_early(turn, carry):
        fits, k, l, i, j = place_of(turn)

        @pl.when(fits & (k < major - 1))
        def _():
            settle(i * minor + j, i, j)

        return carry

    def settle_late(l, carry):
        i, j = nearest(a, major, jnp.int32(major - 1)), nearest(b, minor, l)
        settle(i * minor + j, i, j)
        return carry

    lax.fori_loop(0, rounds, one_shard, 0)
    lax.fori_loop(0, minor, settle_late, 0)
    for turn in range(1, tp_size):
        for k in range(per_peer):
            for h in range(kv_local):
                swap(turn, k, h).wait()


def copy_out(attended, log_norm, attended_out, log_norm_out, sems):
    copies = [
        pltpu.make_async_copy(log_norm, log_norm_out, sems.at[0]),
        pltpu.make_async_copy(attended, attended_out, sems.at[1]),
    ]
    for copy in copies:
        copy.start()
    for copy in copies:
        copy.wait()


def body(tp_size, ctx_size, queries, rotated_key_rows, ordered_value_rows, block_order, live_blocks):
    tok_rows, own_columns = queries.shape
    kv_columns = rotated_key_rows.shape[1]
    kv_local = kv_columns // HEAD_SIZE
    heads_local = own_columns // HEAD_SIZE
    groups = heads_local // kv_local
    blocks_here = tok_rows // BLOCK_TOKENS
    width = groups * BLOCK_TOKENS
    major, minor = grid_of(ctx_size)
    parts = 2 if blocks_here % 2 == 0 else 1
    dims = (major, minor, tp_size, kv_local, groups, blocks_here, parts, live_blocks.shape[1])
    per_peer = blocks_here // tp_size
    per_part = blocks_here // parts
    whole = pl.BlockSpec(memory_space=pltpu.VMEM)
    small = pl.BlockSpec(memory_space=pltpu.SMEM)
    apart = pl.BlockSpec(memory_space=pl.ANY)
    attended, log_norm = pl.pallas_call(
        functools.partial(kernel, dims),
        out_shape=(
            pltpu.VMEM((tok_rows // tp_size, own_columns * tp_size), jnp.bfloat16),
            pltpu.VMEM((heads_local, tok_rows), jnp.float32),
        ),
        in_specs=[apart, apart, apart, small, small],
        out_specs=(whole, whole),
        scratch_shapes=[
            pltpu.VMEM(
                (ctx_size, parts, kv_local, per_part, 2, BLOCK_TOKENS, HEAD_SIZE), jnp.bfloat16
            ),
            pltpu.VMEM((tok_rows, own_columns), jnp.bfloat16),
            pltpu.VMEM((blocks_here, kv_local, HEAD_SIZE, width), jnp.bfloat16),
            pltpu.VMEM((blocks_here, kv_local, HEAD_SIZE, width), jnp.float32),
            pltpu.VMEM((blocks_here, kv_local, 1, width), jnp.float32),
            pltpu.VMEM((blocks_here, kv_local, 1, width), jnp.float32),
            pltpu.VMEM((blocks_here, BLOCK_TOKENS, own_columns), jnp.bfloat16),
            pltpu.SMEM((2, blocks_here * blocks_here), jnp.float32),
            pltpu.VMEM((SLOTS, tok_rows, CHUNK), jnp.float32),
            pltpu.SemaphoreType.DMA((parts + 1, kv_local, per_part, 2)),
            pltpu.SemaphoreType.DMA((ctx_size, parts, 4)),
            pltpu.SemaphoreType.DMA((ctx_size, parts, kv_local)),
            pltpu.SemaphoreType.DMA((tp_size - 1, per_peer, kv_local)),
            pltpu.SemaphoreType.DMA((tp_size - 1, per_peer, kv_local)),
        ],
        compiler_params=pltpu.CompilerParams(collective_id=0, has_side_effects=True),
        name="gather_attend",
    )(queries, rotated_key_rows, ordered_value_rows, block_order.reshape(1, -1), live_blocks)
    return pl.pallas_call(
        copy_out,
        out_shape=(
            jax.ShapeDtypeStruct(attended.shape, attended.dtype),
            jax.ShapeDtypeStruct(log_norm.shape, log_norm.dtype),
        ),
        in_specs=[whole, whole],
        out_specs=(apart, apart),
        scratch_shapes=[pltpu.SemaphoreType.DMA((2,))],
        name="copy_out",
    )(
        pltpu.with_memory_space_constraint(attended, pltpu.VMEM),
        pltpu.with_memory_space_constraint(log_norm, pltpu.VMEM),
    )


def solution(mesh):
    placed = (
        P(("rep", "ctx"), "tp"),
        P(("rep", "ctx"), "tp"),
        P(("rep", "ctx"), "tp"),
        P("rep"),
        P("rep", None),
    )
    return jax.shard_map(
        functools.partial(body, mesh.shape["tp"], mesh.shape["ctx"]),
        mesh=mesh,
        in_specs=placed,
        out_specs=(P(("rep", "ctx", "tp"), None), P(("rep", "tp"), "ctx")),
        check_vma=False,
    )
```

time: 36.4 us -> 35.5 us (0.975)
  the two profiles are of different devices: /device:TPU:26 before, /device:TPU:0 now
where the time goes in v1:
time: 35.5 us; the launch traced here: 35.3 us
  Pallas kernels  34.6 us (97%)
  between operations  0.64 us (2%)
    pallas_call x1, Pallas kernels, body(): pl.pallas_call(functools.partial(kernel, dims), out_shape=(pltpu.VMEM((to...  33.6 us
    pallas_call x1, Pallas kernels, body(): pl.pallas_call(copy_out, out_shape=(jax.ShapeDtypeStruct(attended.shape,...  0.99 us

profile of v1, /device:TPU:0, one launch (start us, length us, event | category | flops | bytes accessed | tf_op | source)
XLA Modules:
  0.0 35.3 jit_solution(3105087136861723501)
XLA Ops:
  0.6 33.6 %gather_attend.1 = (bf16[128,4096]{1,0:T(8,128)(2,1)S(1)}, f32[16,256]{1,0:T(8,128)S(1)}) custom-call(bf16[256,2048]{1,0:T(8,128)(2,1)} %queries.1, bf16[256,256]{1,0:T(8,128)(2,1)} %keys.1, bf16[256,256]{1,0:T(8,128)(2,1)} %values.1, s32[1,16]{1,0:T(1,128)} %bitcast.1, s32[16,12]{1,0:T(8,128)} %live_blocks.1), custom_call_target="tpu_custom_call" | custom-call | tf_op jit(solution)/shard_map/gather_attend/pallas_call | solution.py:373
  34.3 1.0 %copy_out.1 = (bf16[128,4096]{1,0:T(8,128)(2,1)}, f32[16,256]{1,0:T(8,128)}) custom-call(bf16[128,4096]{1,0:T(8,128)(2,1)S(1)} %get-tuple-element.4.attended, f32[16,256]{1,0:T(8,128)S(1)} %get-tuple-element.5.log_norm), custom_call_target="tpu_custom_call" | custom-call | tf_op jit(solution)/shard_map/copy_out/pallas_call | solution.py:402

commit v2 on v1

--- a/solution.py
+++ b/solution.py
@@ -33,6 +33,9 @@
     attended,
     log_norm,
     held,
+    own,
+    order,
+    live,
     raw_queries,
     turned_queries,
     total,
@@ -56,23 +59,15 @@
     mine = lax.axis_index("tp")
     a, b = me // minor, me % minor
 
-    loads = {}
-    for part in range(parts):
-        for h in range(kv_local):
-            for kb in range(per_part):
-                at = pl.ds((part * per_part + kb) * BLOCK_TOKENS, BLOCK_TOKENS)
-                lanes = pl.ds(h * HEAD_SIZE, HEAD_SIZE)
-                for kind, source in enumerate((keys, values)):
-                    loads[part, h, kb, kind] = pltpu.make_async_copy(
-                        source.at[at, lanes],
-                        held.at[me, part, h, kb, kind],
-                        load_sem.at[part, h, kb, kind],
-                    )
-    for load in loads.values():
-        load.start()
-    load_queries = pltpu.make_async_copy(queries, raw_queries, load_sem.at[parts, 0, 0, 0])
-    load_queries.start()
-
+    tables = [
+        pltpu.make_async_copy(block_order, order, load_sem.at[0]),
+        pltpu.make_async_copy(live_blocks, live, load_sem.at[1]),
+    ]
+    loads = [
+        pltpu.make_async_copy(keys, own.at[0], load_sem.at[2]),
+        pltpu.make_async_copy(values, own.at[1], load_sem.at[3]),
+        pltpu.make_async_copy(queries, raw_queries, load_sem.at[4]),
+    ]
     barrier = pltpu.get_barrier_semaphore()
     sides = (
         (a > 0, me - minor),
@@ -89,6 +84,8 @@
     for turn in range(1, tp_size):
         peer = (mine + turn) % tp_size
         pl.semaphore_signal(barrier, inc=1, device_id={"tp": peer}, device_id_type=MESH)
+    for load in tables + loads:
+        load.start()
     expected = jnp.int32(tp_size - 1)
     for there, _ in sides:
         expected = expected + there.astype(jnp.int32)
@@ -120,6 +117,23 @@
                     device_id_type=MESH,
                 ).start()
 
+    def send_own(part, h):
+        for side, wanted in enumerate(onward(part, a, b)):
+
+            @pl.when(wanted)
+            def _(side=side):
+                for kb in range(per_part):
+                    at = pl.ds((part * per_part + kb) * BLOCK_TOKENS, BLOCK_TOKENS)
+                    for kind, source in enumerate((keys, values)):
+                        pltpu.make_async_remote_copy(
+                            src_ref=source.at[at, pl.ds(h * HEAD_SIZE, HEAD_SIZE)],
+                            dst_ref=held.at[me, part, h, kb, kind],
+                            send_sem=send_sem.at[me, part, side],
+                            recv_sem=recv_sem.at[me, part, h],
+                            device_id={"ctx": sides[side][1]},
+                            device_id_type=MESH,
+                        ).start()
+
     def settle(slot, i, j):
         for part in range(parts):
             for side, wanted in enumerate(onward(part, i, j)):
@@ -130,32 +144,38 @@
                         held.at[slot, part], held.at[slot, part], send_sem.at[slot, part, side]
                     ).wait()
 
-    def find_limits(slot):
+    def find_limits(slot, carry):
         for query_block in range(blocks_here):
-            my_seq = block_order[0, me * blocks_here + query_block]
+            my_seq = order[0, me * blocks_here + query_block]
             found = [jnp.bool_(False)] * blocks_here
-            names = [block_order[0, slot * blocks_here + kb] for kb in range(blocks_here)]
+            names = [order[0, slot * blocks_here + kb] for kb in range(blocks_here)]
             for entry in range(slots_live):
-                listed = live_blocks[my_seq, entry]
+                listed = live[my_seq, entry]
                 found = [f | (listed == name) for f, name in zip(found, names)]
             for kb in range(blocks_here):
-                limits[0, query_block * blocks_here + kb] = jnp.where(found[kb], HUGE, -FAR)
-                limits[1, query_block * blocks_here + kb] = jnp.where(found[kb], -HUGE, FAR)
-
-    def attend(slot, h, own):
+                limits[slot, query_block, kb] = jnp.where(found[kb], HUGE, -FAR)
+        return carry
+
+    def attend(slot, h, first, after=None):
+        if first:
+            lanes = pl.ds(pl.multiple_of(h * HEAD_SIZE, HEAD_SIZE), HEAD_SIZE)
+            keys_here, values_here = own[0, :, lanes], own[1, :, lanes]
+        else:
+            blocks = [(kb // per_part, kb % per_part) for kb in range(blocks_here)]
+            keys_here, values_here = (
+                jnp.concatenate([held[slot, part, h, kb, kind] for part, kb in blocks], axis=0)
+                for kind in range(2)
+            )
+        turned_values = jnp.transpose(values_here)
+        turned = (mine + 1) * per_peer
         units = [
-            (query_block, start)
-            for query_block in range(blocks_here)
+            (q if first else (turned + q) % blocks_here, q, start)
+            for q in range(blocks_here)
             for start in range(0, width, CHUNK)
         ]
-        blocks = [(kb // per_part, kb % per_part) for kb in range(blocks_here)]
-        keys_here = jnp.concatenate([held[slot, part, h, kb, 0] for part, kb in blocks], axis=0)
-        turned_values = jnp.transpose(
-            jnp.concatenate([held[slot, part, h, kb, 1] for part, kb in blocks], axis=0)
-        )
 
         def score(u):
-            query_block, start = units[u]
+            query_block, q, start = units[u]
             part = jnp.dot(
                 keys_here,
                 turned_queries[query_block, h, :, pl.ds(start, CHUNK)],
@@ -164,7 +184,7 @@
             tops = []
             for kb in range(blocks_here):
                 block = part[kb * BLOCK_TOKENS : (kb + 1) * BLOCK_TOKENS]
-                if own and kb == query_block:
+                if first and kb == q:
                     key_at = lax.broadcasted_iota(jnp.int32, block.shape, 0)
                     row_at = lax.broadcasted_iota(jnp.int32, block.shape, 1) % BLOCK_TOKENS
                     block = jnp.where(key_at <= row_at, block, -FAR)
@@ -173,14 +193,13 @@
             return tops
 
         def absorb(u, tops):
-            query_block, start = units[u]
+            query_block, q, start = units[u]
             lanes = pl.ds(start, CHUNK)
-            first = query_block * blocks_here
             new_peak = None
             for kb, top in enumerate(tops):
-                top = jnp.minimum(top, limits[0, first + kb])
+                top = jnp.minimum(top, limits[slot, query_block, kb])
                 new_peak = top if new_peak is None else jnp.maximum(new_peak, top)
-            if not own:
+            if not first:
                 old_peak = peak[query_block, h, :, lanes]
                 new_peak = jnp.maximum(new_peak, old_peak)
             peak[query_block, h, :, lanes] = new_peak
@@ -188,7 +207,7 @@
             added = None
             low = []
             for kb in range(blocks_here):
-                floor = jnp.maximum(level, limits[1, first + kb])
+                floor = jnp.maximum(level, -limits[slot, query_block, kb])
                 for at in range(kb * BLOCK_TOKENS, (kb + 1) * BLOCK_TOKENS, STRIP):
                     w = jnp.exp2(scores[u % SLOTS, pl.ds(at, STRIP), :] * scale - floor)
                     added = w if added is None else added + w
@@ -199,7 +218,7 @@
                 jnp.concatenate(low, axis=0),
                 preferred_element_type=jnp.float32,
             )
-            if own:
+            if first:
                 weight_sum[query_block, h, :, lanes] = added
                 total[query_block, h, :, lanes] = product
             else:
@@ -214,13 +233,15 @@
             if u + SLOTS - 1 < len(units):
                 waiting.append(score(u + SLOTS - 1))
             absorb(u, waiting[u])
+            if after is not None and (u + 1) % (len(units) // blocks_here) == 0:
+                after(units[u][1])
 
     per_peer = blocks_here // tp_size
     wide = kv_local * width
 
     def swap(turn, k, h):
         peer = (mine + turn) % tp_size
-        source = pl.ds(h * width, width)
+        source = pl.ds(pl.multiple_of(h * width, HEAD_SIZE), width)
         target = pl.ds(pl.multiple_of(mine * wide + h * width, HEAD_SIZE), width)
         return pltpu.make_async_remote_copy(
             src_ref=leaving.at[peer * per_peer + k, :, source],
@@ -231,38 +252,35 @@
             device_id_type=MESH,
         )
 
-    def finish(h):
-        for turn in range(1, tp_size + 1):
-            peer = (mine + turn) % tp_size
-            for k in range(per_peer):
-                query_block = peer * per_peer + k
-                at = pl.ds(pl.multiple_of(query_block * BLOCK_TOKENS, BLOCK_TOKENS), BLOCK_TOKENS)
-                for g in range(groups):
-                    head = h * groups + g
-                    lanes = pl.ds(g * BLOCK_TOKENS, BLOCK_TOKENS)
-                    bottom = weight_sum[query_block, h, :, lanes]
-                    normed = total[query_block, h, :, lanes] * (1.0 / bottom)
-                    tile = jnp.transpose(normed.astype(jnp.bfloat16))
-                    if turn < tp_size:
-                        leaving[query_block, :, pl.ds(head * HEAD_SIZE, HEAD_SIZE)] = tile
-                    else:
-                        to = pl.multiple_of(mine * wide + head * HEAD_SIZE, HEAD_SIZE)
-                        attended[pl.ds(k * BLOCK_TOKENS, BLOCK_TOKENS), pl.ds(to, HEAD_SIZE)] = tile
-                    log_norm[pl.ds(head, 1), at] = (
-                        peak[query_block, h, :, lanes] * factor + jnp.log(bottom)
-                    )
-                if turn < tp_size:
-                    swap(turn, k, h).start()
-
-    for part in range(parts):
-        for h in range(kv_local):
-            for kb in range(per_part):
-                for kind in range(2):
-                    loads[part, h, kb, kind].wait()
+    def finish(h, q):
+        turn, k = 1 + q // per_peer, q % per_peer
+        peer = (mine + turn) % tp_size
+        query_block = peer * per_peer + k
+        at = pl.ds(pl.multiple_of(query_block * BLOCK_TOKENS, BLOCK_TOKENS), BLOCK_TOKENS)
+        norms = []
+        for g in range(groups):
+            head = h * groups + g
+            lanes = pl.ds(g * BLOCK_TOKENS, BLOCK_TOKENS)
+            bottom = weight_sum[query_block, h, :, lanes]
+            normed = total[query_block, h, :, lanes] * (1.0 / bottom)
+            tile = jnp.transpose(normed.astype(jnp.bfloat16))
+            if turn < tp_size:
+                to = pl.multiple_of(head * HEAD_SIZE, HEAD_SIZE)
+                leaving[query_block, :, pl.ds(to, HEAD_SIZE)] = tile
+            else:
+                to = pl.multiple_of(mine * wide + head * HEAD_SIZE, HEAD_SIZE)
+                attended[pl.ds(k * BLOCK_TOKENS, BLOCK_TOKENS), pl.ds(to, HEAD_SIZE)] = tile
+            norms.append(peak[query_block, h, :, lanes] * factor + jnp.log(bottom))
+        heads = pl.ds(pl.multiple_of(h * groups, groups), groups)
+        log_norm[heads, at] = jnp.concatenate(norms, axis=0)
+        if turn < tp_size:
+            swap(turn, k, h).start()
+
     for h in range(kv_local):
         for part in range(parts):
-            send_on(me, part, h, a, b)
-    load_queries.wait()
+            send_own(part, h)
+    for load in tables + loads:
+        load.wait()
 
     def turn_block(query_block, carry):
         at = pl.ds(pl.multiple_of(query_block * BLOCK_TOKENS, BLOCK_TOKENS), BLOCK_TOKENS)
@@ -275,9 +293,14 @@
         return carry
 
     lax.fori_loop(0, blocks_here, turn_block, 0)
-    find_limits(me)
-    for h in range(kv_local):
+    lax.fori_loop(me, me + 1, find_limits, 0)
+
+    def attend_own(h, carry):
         attend(me, h, True)
+        return carry
+
+    lax.fori_loop(0, kv_local, attend_own, 0)
+    lax.fori_loop(0, major * minor, find_limits, 0)
 
     def nearest(x, n, k):
         both = jnp.minimum(x, n - 1 - x)
@@ -286,57 +309,54 @@
         return x + away * jnp.where(k <= 2 * both, paired, k - both)
 
     lag = 1 + ((a > 0) & (a < major - 1)).astype(jnp.int32)
-
-    def place_of(turn):
-        l = turn % minor
-        k = turn // minor - lag * l
-        fits = (k >= 0) & (k < major)
-        return fits, k, l, nearest(a, major, k), nearest(b, minor, l)
-
-    rounds = (major + 2 * (minor - 1)) * minor
-
-    def one_shard(turn, carry):
-        fits, k, l, i, j = place_of(turn)
+    waves = major - 1 + lag * (minor - 1)
+
+    def place_of(wave, l):
+        k = wave - lag * l
+        return (k >= 0) & (k < major), k, nearest(a, major, k), nearest(b, minor, l)
+
+    def take(slot, h, i, j):
+        for part in range(parts):
+            pltpu.make_async_copy(
+                held.at[slot, part, h], held.at[slot, part, h], recv_sem.at[slot, part, h]
+            ).wait()
+            send_on(slot, part, h, i, j)
+
+    def one_turn(turn, carry):
+        l, h = turn % minor, (turn // minor) % kv_local
+        fits, k, i, j = place_of(turn // (minor * kv_local), l)
         slot = i * minor + j
-        last = (k == major - 1) & (l == minor - 1)
 
         @pl.when(fits & (k + l > 0))
         def _():
-            @pl.when(last)
-            def _():
-                lax.fori_loop(0, rounds, settle_early, 0)
-
-            find_limits(slot)
-            for h in range(kv_local):
-                for part in range(parts):
-                    pltpu.make_async_copy(
-                        held.at[slot, part, h], held.at[slot, part, h], recv_sem.at[slot, part, h]
-                    ).wait()
-                    send_on(slot, part, h, i, j)
-                attend(slot, h, False)
-
-                @pl.when(last)
-                def _(h=h):
-                    finish(h)
-
-        return carry
-
-    def settle_early(turn, carry):
-        fits, k, l, i, j = place_of(turn)
-
-        @pl.when(fits & (k < major - 1))
+            take(slot, h, i, j)
+            attend(slot, h, False)
+
+        return carry
+
+    lax.fori_loop(kv_local * minor, waves * kv_local * minor, one_turn, 0)
+
+    def settle_one(turn, carry):
+        fits, _, i, j = place_of(turn // minor, turn % minor)
+
+        @pl.when(fits)
         def _():
             settle(i * minor + j, i, j)
 
         return carry
 
-    def settle_late(l, carry):
-        i, j = nearest(a, major, jnp.int32(major - 1)), nearest(b, minor, l)
-        settle(i * minor + j, i, j)
-        return carry
-
-    lax.fori_loop(0, rounds, one_shard, 0)
-    lax.fori_loop(0, minor, settle_late, 0)
+    early = (waves - lag) * minor
+    lax.fori_loop(0, early, settle_one, 0)
+    far_i, far_j = nearest(a, major, jnp.int32(major - 1)), nearest(b, minor, jnp.int32(minor - 1))
+
+    def last_turn(h, carry):
+        slot = far_i * minor + far_j
+        take(slot, h, far_i, far_j)
+        attend(slot, h, False, functools.partial(finish, h))
+        return carry
+
+    lax.fori_loop(0, kv_local, last_turn, 0)
+    lax.fori_loop(early, (waves + 1) * minor, settle_one, 0)
     for turn in range(1, tp_size):
         for k in range(per_peer):
             for h in range(kv_local):
@@ -368,7 +388,6 @@
     per_peer = blocks_here // tp_size
     per_part = blocks_here // parts
     whole = pl.BlockSpec(memory_space=pltpu.VMEM)
-    small = pl.BlockSpec(memory_space=pltpu.SMEM)
     apart = pl.BlockSpec(memory_space=pl.ANY)
     attended, log_norm = pl.pallas_call(
         functools.partial(kernel, dims),
@@ -376,21 +395,24 @@
             pltpu.VMEM((tok_rows // tp_size, own_columns * tp_size), jnp.bfloat16),
             pltpu.VMEM((heads_local, tok_rows), jnp.float32),
         ),
-        in_specs=[apart, apart, apart, small, small],
+        in_specs=[apart] * 5,
         out_specs=(whole, whole),
         scratch_shapes=[
             pltpu.VMEM(
                 (ctx_size, parts, kv_local, per_part, 2, BLOCK_TOKENS, HEAD_SIZE), jnp.bfloat16
             ),
+            pltpu.VMEM((2, tok_rows, kv_columns), jnp.bfloat16),
+            pltpu.SMEM((1, block_order.shape[0]), jnp.int32),
+            pltpu.SMEM(live_blocks.shape, jnp.int32),
             pltpu.VMEM((tok_rows, own_columns), jnp.bfloat16),
             pltpu.VMEM((blocks_here, kv_local, HEAD_SIZE, width), jnp.bfloat16),
             pltpu.VMEM((blocks_here, kv_local, HEAD_SIZE, width), jnp.float32),
             pltpu.VMEM((blocks_here, kv_local, 1, width), jnp.float32),
             pltpu.VMEM((blocks_here, kv_local, 1, width), jnp.float32),
             pltpu.VMEM((blocks_here, BLOCK_TOKENS, own_columns), jnp.bfloat16),
-            pltpu.SMEM((2, blocks_here * blocks_here), jnp.float32),
+            pltpu.SMEM((ctx_size, blocks_here, blocks_here), jnp.float32),
             pltpu.VMEM((SLOTS, tok_rows, CHUNK), jnp.float32),
-            pltpu.SemaphoreType.DMA((parts + 1, kv_local, per_part, 2)),
+            pltpu.SemaphoreType.DMA((5,)),
             pltpu.SemaphoreType.DMA((ctx_size, parts, 4)),
             pltpu.SemaphoreType.DMA((ctx_size, parts, kv_local)),
             pltpu.SemaphoreType.DMA((tp_size - 1, per_peer, kv_local)),

time: 35.5 us -> 34 us (0.958)
  Pallas kernels: 34.6 us -> 33.2 us
    pallas_call x1, Pallas kernels: 33.6 us -> 32.2 us  [body(): pl.pallas_call(functools.partial(kernel, dims), out_shape=(pltpu.VMEM((to...]
where the time goes in v2:
time: 34 us; the launch traced here: 33.9 us
  Pallas kernels  33.2 us (98%)
  between operations  0.64 us (2%)
    pallas_call x1, Pallas kernels, body(): pl.pallas_call(functools.partial(kernel, dims), out_shape=(pltpu.VMEM((to...  32.2 us
    pallas_call x1, Pallas kernels, body(): pl.pallas_call(copy_out, out_shape=(jax.ShapeDtypeStruct(attended.shape,...  0.99 us

profile of v2, /device:TPU:0, one launch (start us, length us, event | category | flops | bytes accessed | tf_op | source)
XLA Modules:
  0.0 33.9 jit_solution(15272281184231144162)
XLA Ops:
  0.6 32.2 %gather_attend.1 = (bf16[128,4096]{1,0:T(8,128)(2,1)S(1)}, f32[16,256]{1,0:T(8,128)S(1)}) custom-call(bf16[256,2048]{1,0:T(8,128)(2,1)} %queries.1, bf16[256,256]{1,0:T(8,128)(2,1)} %keys.1, bf16[256,256]{1,0:T(8,128)(2,1)} %values.1, s32[1,16]{1,0:T(1,128)} %bitcast.1, s32[16,12]{1,0:T(8,128)} %live_blocks.1), custom_call_target="tpu_custom_call" | custom-call | tf_op jit(solution)/shard_map/gather_attend/pallas_call | solution.py:392
  32.9 1.0 %copy_out.1 = (bf16[128,4096]{1,0:T(8,128)(2,1)}, f32[16,256]{1,0:T(8,128)}) custom-call(bf16[128,4096]{1,0:T(8,128)(2,1)S(1)} %get-tuple-element.4.attended, f32[16,256]{1,0:T(8,128)S(1)} %get-tuple-element.5.log_norm), custom_call_target="tpu_custom_call" | custom-call | tf_op jit(solution)/shard_map/copy_out/pallas_call | solution.py:424

commit v3 on v2

--- a/solution.py
+++ b/solution.py
@@ -50,11 +50,13 @@
     swap_send,
     swap_recv,
 ):
-    major, minor, tp_size, kv_local, groups, blocks_here, parts, slots_live = dims
+    major, minor, tp_size, kv_local, groups, blocks_here, cut, slots_live = dims
     factor = HEAD_SIZE ** (-0.5)
     scale = factor * math.log2(math.e)
     width = groups * BLOCK_TOKENS
-    per_part = blocks_here // parts
+    rows = blocks_here * BLOCK_TOKENS
+    spans = [pl.ds(0, cut), pl.ds(cut, rows - cut)]
+    parts = len(spans)
     me = lax.axis_index("ctx")
     mine = lax.axis_index("tp")
     a, b = me // minor, me % minor
@@ -93,7 +95,7 @@
 
     def onward(part, i, j):
         column_first = j == b
-        row_first = (i == 0) | (i == major - 1) if part == parts - 1 and parts > 1 else jnp.bool_(False)
+        row_first = (i == 0) | (i == major - 1) if part == parts - 1 else jnp.bool_(False)
         along = column_first | row_first
         across = (i == a) | jnp.logical_not(row_first)
         return (
@@ -109,8 +111,8 @@
             @pl.when(wanted)
             def _(side=side):
                 pltpu.make_async_remote_copy(
-                    src_ref=held.at[slot, part, h],
-                    dst_ref=held.at[slot, part, h],
+                    src_ref=held.at[slot, h, :, spans[part]],
+                    dst_ref=held.at[slot, h, :, spans[part]],
                     send_sem=send_sem.at[slot, part, side],
                     recv_sem=recv_sem.at[slot, part, h],
                     device_id={"ctx": sides[side][1]},
@@ -122,17 +124,15 @@
 
             @pl.when(wanted)
             def _(side=side):
-                for kb in range(per_part):
-                    at = pl.ds((part * per_part + kb) * BLOCK_TOKENS, BLOCK_TOKENS)
-                    for kind, source in enumerate((keys, values)):
-                        pltpu.make_async_remote_copy(
-                            src_ref=source.at[at, pl.ds(h * HEAD_SIZE, HEAD_SIZE)],
-                            dst_ref=held.at[me, part, h, kb, kind],
-                            send_sem=send_sem.at[me, part, side],
-                            recv_sem=recv_sem.at[me, part, h],
-                            device_id={"ctx": sides[side][1]},
-                            device_id_type=MESH,
-                        ).start()
+                for kind, source in enumerate((keys, values)):
+                    pltpu.make_async_remote_copy(
+                        src_ref=source.at[spans[part], pl.ds(h * HEAD_SIZE, HEAD_SIZE)],
+                        dst_ref=held.at[me, h, kind, spans[part]],
+                        send_sem=send_sem.at[me, part, side],
+                        recv_sem=recv_sem.at[me, part, h],
+                        device_id={"ctx": sides[side][1]},
+                        device_id_type=MESH,
+                    ).start()
 
     def settle(slot, i, j):
         for part in range(parts):
@@ -141,7 +141,9 @@
                 @pl.when(wanted)
                 def _(part=part, side=side):
                     pltpu.make_async_copy(
-                        held.at[slot, part], held.at[slot, part], send_sem.at[slot, part, side]
+                        held.at[slot, :, :, spans[part]],
+                        held.at[slot, :, :, spans[part]],
+                        send_sem.at[slot, part, side],
                     ).wait()
 
     def find_limits(slot, carry):
@@ -161,11 +163,7 @@
             lanes = pl.ds(pl.multiple_of(h * HEAD_SIZE, HEAD_SIZE), HEAD_SIZE)
             keys_here, values_here = own[0, :, lanes], own[1, :, lanes]
         else:
-            blocks = [(kb // per_part, kb % per_part) for kb in range(blocks_here)]
-            keys_here, values_here = (
-                jnp.concatenate([held[slot, part, h, kb, kind] for part, kb in blocks], axis=0)
-                for kind in range(2)
-            )
+            keys_here, values_here = held[slot, h, 0], held[slot, h, 1]
         turned_values = jnp.transpose(values_here)
         turned = (mine + 1) * per_peer
         units = [
@@ -308,36 +306,41 @@
         paired = ((k + 1) // 2) * (2 * (k % 2) - 1)
         return x + away * jnp.where(k <= 2 * both, paired, k - both)
 
-    lag = 1 + ((a > 0) & (a < major - 1)).astype(jnp.int32)
-    waves = major - 1 + lag * (minor - 1)
-
-    def place_of(wave, l):
-        k = wave - lag * l
-        return (k >= 0) & (k < major), k, nearest(a, major, k), nearest(b, minor, l)
-
-    def take(slot, h, i, j):
-        for part in range(parts):
+    away = 1 - 2 * (2 * a > major - 1).astype(jnp.int32)
+    far_i, far_j = (away > 0) * (major - 1), (2 * b <= minor - 1) * (minor - 1)
+    waves = jnp.maximum(a, major - 1 - a) + jnp.maximum(b, minor - 1 - b)
+
+    def place_of(wave, turn):
+        j = nearest(b, minor, turn // 2)
+        reach = wave - jnp.abs(j - b)
+        i = a + reach * away * (1 - 2 * (turn % 2))
+        fits = (i >= 0) & (i < major) & ((reach > 0) | ((reach == 0) & (turn % 2 == 0)))
+        return fits & ((i != far_i) | (j != far_j)), i, j
+
+    def take(slot, h, i, j, order):
+        for part in order:
             pltpu.make_async_copy(
-                held.at[slot, part, h], held.at[slot, part, h], recv_sem.at[slot, part, h]
+                held.at[slot, h, :, spans[part]],
+                held.at[slot, h, :, spans[part]],
+                recv_sem.at[slot, part, h],
             ).wait()
             send_on(slot, part, h, i, j)
 
     def one_turn(turn, carry):
-        l, h = turn % minor, (turn // minor) % kv_local
-        fits, k, i, j = place_of(turn // (minor * kv_local), l)
-        slot = i * minor + j
-
-        @pl.when(fits & (k + l > 0))
+        h = (turn // (2 * minor)) % kv_local
+        fits, i, j = place_of(turn // (2 * minor * kv_local), turn % (2 * minor))
+
+        @pl.when(fits)
         def _():
-            take(slot, h, i, j)
-            attend(slot, h, False)
-
-        return carry
-
-    lax.fori_loop(kv_local * minor, waves * kv_local * minor, one_turn, 0)
+            take(i * minor + j, h, i, j, range(parts))
+            attend(i * minor + j, h, False)
+
+        return carry
+
+    lax.fori_loop(2 * minor * kv_local, (waves + 1) * 2 * minor * kv_local, one_turn, 0)
 
     def settle_one(turn, carry):
-        fits, _, i, j = place_of(turn // minor, turn % minor)
+        fits, i, j = place_of(turn // (2 * minor), turn % (2 * minor))
 
         @pl.when(fits)
         def _():
@@ -345,18 +348,18 @@
 
         return carry
 
-    early = (waves - lag) * minor
+    early = (waves - 1) * 2 * minor
     lax.fori_loop(0, early, settle_one, 0)
-    far_i, far_j = nearest(a, major, jnp.int32(major - 1)), nearest(b, minor, jnp.int32(minor - 1))
 
     def last_turn(h, carry):
         slot = far_i * minor + far_j
-        take(slot, h, far_i, far_j)
+        take(slot, h, far_i, far_j, reversed(range(parts)))
         attend(slot, h, False, functools.partial(finish, h))
         return carry
 
     lax.fori_loop(0, kv_local, last_turn, 0)
-    lax.fori_loop(early, (waves + 1) * minor, settle_one, 0)
+    lax.fori_loop(early, (waves + 1) * 2 * minor, settle_one, 0)
+    settle(far_i * minor + far_j, far_i, far_j)
     for turn in range(1, tp_size):
         for k in range(per_peer):
             for h in range(kv_local):
@@ -383,10 +386,9 @@
     blocks_here = tok_rows // BLOCK_TOKENS
     width = groups * BLOCK_TOKENS
     major, minor = grid_of(ctx_size)
-    parts = 2 if blocks_here % 2 == 0 else 1
-    dims = (major, minor, tp_size, kv_local, groups, blocks_here, parts, live_blocks.shape[1])
+    cut = tok_rows // 2
+    dims = (major, minor, tp_size, kv_local, groups, blocks_here, cut, live_blocks.shape[1])
     per_peer = blocks_here // tp_size
-    per_part = blocks_here // parts
     whole = pl.BlockSpec(memory_space=pltpu.VMEM)
     apart = pl.BlockSpec(memory_space=pl.ANY)
     attended, log_norm = pl.pallas_call(
@@ -398,9 +400,7 @@
         in_specs=[apart] * 5,
         out_specs=(whole, whole),
         scratch_shapes=[
-            pltpu.VMEM(
-                (ctx_size, parts, kv_local, per_part, 2, BLOCK_TOKENS, HEAD_SIZE), jnp.bfloat16
-            ),
+            pltpu.VMEM((ctx_size, kv_local, 2, tok_rows, HEAD_SIZE), jnp.bfloat16),
             pltpu.VMEM((2, tok_rows, kv_columns), jnp.bfloat16),
             pltpu.SMEM((1, block_order.shape[0]), jnp.int32),
             pltpu.SMEM(live_blocks.shape, jnp.int32),
@@ -413,8 +413,8 @@
             pltpu.SMEM((ctx_size, blocks_here, blocks_here), jnp.float32),
             pltpu.VMEM((SLOTS, tok_rows, CHUNK), jnp.float32),
             pltpu.SemaphoreType.DMA((5,)),
-            pltpu.SemaphoreType.DMA((ctx_size, parts, 4)),
-            pltpu.SemaphoreType.DMA((ctx_size, parts, kv_local)),
+            pltpu.SemaphoreType.DMA((ctx_size, 2, 4)),
+            pltpu.SemaphoreType.DMA((ctx_size, 2, kv_local)),
             pltpu.SemaphoreType.DMA((tp_size - 1, per_peer, kv_local)),
             pltpu.SemaphoreType.DMA((tp_size - 1, per_peer, kv_local)),
         ],

time: 34 us -> 32.7 us (0.962)
  Pallas kernels: 33.2 us -> 31.9 us
    pallas_call x1, Pallas kernels: 32.2 us -> 30.9 us  [body(): pl.pallas_call(functools.partial(kernel, dims), out_shape=(pltpu.VMEM((to...]
where the time goes in v3:
time: 32.7 us; the launch traced here: 32.5 us
  Pallas kernels  31.9 us (98%)
  between operations  0.64 us (2%)
    pallas_call x1, Pallas kernels, body(): pl.pallas_call(functools.partial(kernel, dims), out_shape=(pltpu.VMEM((to...  30.9 us
    pallas_call x1, Pallas kernels, body(): pl.pallas_call(copy_out, out_shape=(jax.ShapeDtypeStruct(attended.shape,...  0.99 us

profile of v3, /device:TPU:0, one launch (start us, length us, event | category | flops | bytes accessed | tf_op | source)
XLA Modules:
  0.0 32.5 jit_solution(4301732382884650184)
XLA Ops:
  0.6 30.9 %gather_attend.1 = (bf16[128,4096]{1,0:T(8,128)(2,1)S(1)}, f32[16,256]{1,0:T(8,128)S(1)}) custom-call(bf16[256,2048]{1,0:T(8,128)(2,1)} %queries.1, bf16[256,256]{1,0:T(8,128)(2,1)} %keys.1, bf16[256,256]{1,0:T(8,128)(2,1)} %values.1, s32[1,16]{1,0:T(1,128)} %bitcast.1, s32[16,12]{1,0:T(8,128)} %live_blocks.1), custom_call_target="tpu_custom_call" | custom-call | tf_op jit(solution)/shard_map/gather_attend/pallas_call | solution.py:394
  31.5 1.0 %copy_out.1 = (bf16[128,4096]{1,0:T(8,128)(2,1)}, f32[16,256]{1,0:T(8,128)}) custom-call(bf16[128,4096]{1,0:T(8,128)(2,1)S(1)} %get-tuple-element.4.attended, f32[16,256]{1,0:T(8,128)S(1)} %get-tuple-element.5.log_norm), custom_call_target="tpu_custom_call" | custom-call | tf_op jit(solution)/shard_map/copy_out/pallas_call | solution.py:424

commit v4 on v3

--- a/solution.py
+++ b/solution.py
@@ -33,7 +33,6 @@
     attended,
     log_norm,
     held,
-    own,
     order,
     live,
     raw_queries,
@@ -62,14 +61,17 @@
     a, b = me // minor, me % minor
 
     tables = [
-        pltpu.make_async_copy(block_order, order, load_sem.at[0]),
-        pltpu.make_async_copy(live_blocks, live, load_sem.at[1]),
+        pltpu.make_async_copy(block_order, order, load_sem.at[0, 0, 0]),
+        pltpu.make_async_copy(live_blocks, live, load_sem.at[1, 0, 0]),
     ]
     loads = [
-        pltpu.make_async_copy(keys, own.at[0], load_sem.at[2]),
-        pltpu.make_async_copy(values, own.at[1], load_sem.at[3]),
-        pltpu.make_async_copy(queries, raw_queries, load_sem.at[4]),
+        pltpu.make_async_copy(
+            source.at[:, pl.ds(h * HEAD_SIZE, HEAD_SIZE)], held.at[me, h, kind], load_sem.at[3, h, kind]
+        )
+        for h in range(kv_local)
+        for kind, source in enumerate((keys, values))
     ]
+    load_queries = pltpu.make_async_copy(queries, raw_queries, load_sem.at[2, 0, 0])
     barrier = pltpu.get_barrier_semaphore()
     sides = (
         (a > 0, me - minor),
@@ -86,7 +88,7 @@
     for turn in range(1, tp_size):
         peer = (mine + turn) % tp_size
         pl.semaphore_signal(barrier, inc=1, device_id={"tp": peer}, device_id_type=MESH)
-    for load in tables + loads:
+    for load in loads + [load_queries] + tables:
         load.start()
     expected = jnp.int32(tp_size - 1)
     for there, _ in sides:
@@ -119,21 +121,6 @@
                     device_id_type=MESH,
                 ).start()
 
-    def send_own(part, h):
-        for side, wanted in enumerate(onward(part, a, b)):
-
-            @pl.when(wanted)
-            def _(side=side):
-                for kind, source in enumerate((keys, values)):
-                    pltpu.make_async_remote_copy(
-                        src_ref=source.at[spans[part], pl.ds(h * HEAD_SIZE, HEAD_SIZE)],
-                        dst_ref=held.at[me, h, kind, spans[part]],
-                        send_sem=send_sem.at[me, part, side],
-                        recv_sem=recv_sem.at[me, part, h],
-                        device_id={"ctx": sides[side][1]},
-                        device_id_type=MESH,
-                    ).start()
-
     def settle(slot, i, j):
         for part in range(parts):
             for side, wanted in enumerate(onward(part, i, j)):
@@ -158,35 +145,32 @@
                 limits[slot, query_block, kb] = jnp.where(found[kb], HUGE, -FAR)
         return carry
 
-    def attend(slot, h, first, after=None):
-        if first:
-            lanes = pl.ds(pl.multiple_of(h * HEAD_SIZE, HEAD_SIZE), HEAD_SIZE)
-            keys_here, values_here = own[0, :, lanes], own[1, :, lanes]
-        else:
-            keys_here, values_here = held[slot, h, 0], held[slot, h, 1]
-        turned_values = jnp.transpose(values_here)
+    def attend(slots, h, first, after=None):
+        keys_here = [held[slot, h, 0] for slot in slots]
+        turned_values = jnp.concatenate([jnp.transpose(held[slot, h, 1]) for slot in slots], axis=1)
         turned = (mine + 1) * per_peer
         units = [
             (q if first else (turned + q) % blocks_here, q, start)
             for q in range(blocks_here)
             for start in range(0, width, CHUNK)
         ]
+        blocks = [(n, slot, kb) for n, slot in enumerate(slots) for kb in range(blocks_here)]
 
         def score(u):
             query_block, q, start = units[u]
-            part = jnp.dot(
-                keys_here,
-                turned_queries[query_block, h, :, pl.ds(start, CHUNK)],
-                preferred_element_type=jnp.float32,
-            )
+            turned_here = turned_queries[query_block, h, :, pl.ds(start, CHUNK)]
+            parts = [
+                jnp.dot(k, turned_here, preferred_element_type=jnp.float32) for k in keys_here
+            ]
             tops = []
-            for kb in range(blocks_here):
-                block = part[kb * BLOCK_TOKENS : (kb + 1) * BLOCK_TOKENS]
+            for n, slot, kb in blocks:
+                block = parts[n][kb * BLOCK_TOKENS : (kb + 1) * BLOCK_TOKENS]
                 if first and kb == q:
                     key_at = lax.broadcasted_iota(jnp.int32, block.shape, 0)
                     row_at = lax.broadcasted_iota(jnp.int32, block.shape, 1) % BLOCK_TOKENS
                     block = jnp.where(key_at <= row_at, block, -FAR)
-                scores[u % SLOTS, pl.ds(kb * BLOCK_TOKENS, BLOCK_TOKENS), :] = block
+                at = n * rows + kb * BLOCK_TOKENS
+                scores[u % SLOTS, pl.ds(at, BLOCK_TOKENS), :] = block
                 tops.append(jnp.max(block, axis=0, keepdims=True))
             return tops
 
@@ -194,7 +178,7 @@
             query_block, q, start = units[u]
             lanes = pl.ds(start, CHUNK)
             new_peak = None
-            for kb, top in enumerate(tops):
+            for (n, slot, kb), top in zip(blocks, tops):
                 top = jnp.minimum(top, limits[slot, query_block, kb])
                 new_peak = top if new_peak is None else jnp.maximum(new_peak, top)
             if not first:
@@ -204,9 +188,10 @@
             level = new_peak * scale
             added = None
             low = []
-            for kb in range(blocks_here):
+            for n, slot, kb in blocks:
                 floor = jnp.maximum(level, -limits[slot, query_block, kb])
-                for at in range(kb * BLOCK_TOKENS, (kb + 1) * BLOCK_TOKENS, STRIP):
+                start_at = n * rows + kb * BLOCK_TOKENS
+                for at in range(start_at, start_at + BLOCK_TOKENS, STRIP):
                     w = jnp.exp2(scores[u % SLOTS, pl.ds(at, STRIP), :] * scale - floor)
                     added = w if added is None else added + w
                     low.append(w.astype(jnp.bfloat16))
@@ -274,10 +259,12 @@
         if turn < tp_size:
             swap(turn, k, h).start()
 
+    for load in loads:
+        load.wait()
     for h in range(kv_local):
         for part in range(parts):
-            send_own(part, h)
-    for load in tables + loads:
+            send_on(me, part, h, a, b)
+    for load in [load_queries] + tables:
         load.wait()
 
     def turn_block(query_block, carry):
@@ -294,7 +281,7 @@
     lax.fori_loop(me, me + 1, find_limits, 0)
 
     def attend_own(h, carry):
-        attend(me, h, True)
+        attend([me], h, True)
         return carry
 
     lax.fori_loop(0, kv_local, attend_own, 0)
@@ -306,60 +293,78 @@
         paired = ((k + 1) // 2) * (2 * (k % 2) - 1)
         return x + away * jnp.where(k <= 2 * both, paired, k - both)
 
-    away = 1 - 2 * (2 * a > major - 1).astype(jnp.int32)
-    far_i, far_j = (away > 0) * (major - 1), (2 * b <= minor - 1) * (minor - 1)
-    waves = jnp.maximum(a, major - 1 - a) + jnp.maximum(b, minor - 1 - b)
-
-    def place_of(wave, turn):
-        j = nearest(b, minor, turn // 2)
-        reach = wave - jnp.abs(j - b)
-        i = a + reach * away * (1 - 2 * (turn % 2))
-        fits = (i >= 0) & (i < major) & ((reach > 0) | ((reach == 0) & (turn % 2 == 0)))
-        return fits & ((i != far_i) | (j != far_j)), i, j
-
-    def take(slot, h, i, j, order):
-        for part in order:
-            pltpu.make_async_copy(
-                held.at[slot, h, :, spans[part]],
-                held.at[slot, h, :, spans[part]],
-                recv_sem.at[slot, part, h],
-            ).wait()
-            send_on(slot, part, h, i, j)
-
-    def one_turn(turn, carry):
-        h = (turn // (2 * minor)) % kv_local
-        fits, i, j = place_of(turn // (2 * minor * kv_local), turn % (2 * minor))
-
-        @pl.when(fits)
+    inner = (a > 0) & (a < major - 1)
+    lag = 1 + inner.astype(jnp.int32)
+    both = 2 * (major - 1 - lag)
+
+    def place_of(n):
+        later = n - lag
+        column = (n < lag) | ((later < both) & (later % 2 == 1))
+        k = jnp.where(later < both, later // 2, later - both // 2)
+        k = jnp.where(n < lag, n + 1, k + column * (lag + 1))
+        l = jnp.where(column, 0, 1)
+        if minor > 2:
+            rest = n - (2 * major - 1)
+            k = jnp.where(rest >= 0, rest % major, k)
+            l = jnp.where(rest >= 0, rest // major + 2, l)
+        i, j = nearest(a, major, k), nearest(b, minor, l)
+        return i * minor + j, i, j
+
+    def take_part(slot, part, h, i, j):
+        pltpu.make_async_copy(
+            held.at[slot, h, :, spans[part]],
+            held.at[slot, h, :, spans[part]],
+            recv_sem.at[slot, part, h],
+        ).wait()
+        send_on(slot, part, h, i, j)
+
+    ahead = minor == 2 and major == 4
+
+    def take(place, h):
+        slot, i, j = place
+        for part in range(parts - 1):
+            take_part(slot, part, h, i, j)
+        passed = inner & (j != b) & ((i == 0) | (i == major - 1)) if ahead else jnp.bool_(False)
+
+        @pl.when(jnp.logical_not(passed))
         def _():
-            take(i * minor + j, h, i, j, range(parts))
-            attend(i * minor + j, h, False)
-
-        return carry
-
-    lax.fori_loop(2 * minor * kv_local, (waves + 1) * 2 * minor * kv_local, one_turn, 0)
-
-    def settle_one(turn, carry):
-        fits, i, j = place_of(turn // (2 * minor), turn % (2 * minor))
-
-        @pl.when(fits)
-        def _():
-            settle(i * minor + j, i, j)
-
-        return carry
-
-    early = (waves - 1) * 2 * minor
-    lax.fori_loop(0, early, settle_one, 0)
+            take_part(slot, parts - 1, h, i, j)
+
+    shards = major * minor
+    pairs = (shards - 2) // 2
+    far = place_of(jnp.int32(shards - 2))
+
+    def one_pair(turn, carry):
+        pair, h = turn // kv_local, turn % kv_local
+        here = [place_of(2 * pair + n) for n in range(2)]
+        for place in here:
+            take(place, h)
+        if ahead:
+
+            @pl.when(inner & (pair >= pairs - 2))
+            def _():
+                _, far_i, far_j = far
+                i = jnp.where(pair == pairs - 1, far_i, major - 1 - far_i)
+                take_part(i * minor + far_j, parts - 1, h, i, far_j)
+
+        attend([place[0] for place in here], h, False)
+        return carry
+
+    lax.fori_loop(0, pairs * kv_local, one_pair, 0)
 
     def last_turn(h, carry):
-        slot = far_i * minor + far_j
-        take(slot, h, far_i, far_j, reversed(range(parts)))
-        attend(slot, h, False, functools.partial(finish, h))
+        take(far, h)
+        attend([far[0]], h, False, functools.partial(finish, h))
         return carry
 
     lax.fori_loop(0, kv_local, last_turn, 0)
-    lax.fori_loop(early, (waves + 1) * 2 * minor, settle_one, 0)
-    settle(far_i * minor + far_j, far_i, far_j)
+    settle(me, a, b)
+
+    def settle_one(n, carry):
+        settle(*place_of(n))
+        return carry
+
+    lax.fori_loop(0, shards - 1, settle_one, 0)
     for turn in range(1, tp_size):
         for k in range(per_peer):
             for h in range(kv_local):
@@ -401,7 +406,6 @@
         out_specs=(whole, whole),
         scratch_shapes=[
             pltpu.VMEM((ctx_size, kv_local, 2, tok_rows, HEAD_SIZE), jnp.bfloat16),
-            pltpu.VMEM((2, tok_rows, kv_columns), jnp.bfloat16),
             pltpu.SMEM((1, block_order.shape[0]), jnp.int32),
             pltpu.SMEM(live_blocks.shape, jnp.int32),
             pltpu.VMEM((tok_rows, own_columns), jnp.bfloat16),
@@ -411,8 +415,8 @@
             pltpu.VMEM((blocks_here, kv_local, 1, width), jnp.float32),
             pltpu.VMEM((blocks_here, BLOCK_TOKENS, own_columns), jnp.bfloat16),
             pltpu.SMEM((ctx_size, blocks_here, blocks_here), jnp.float32),
-            pltpu.VMEM((SLOTS, tok_rows, CHUNK), jnp.float32),
-            pltpu.SemaphoreType.DMA((5,)),
+            pltpu.VMEM((SLOTS, 2 * tok_rows, CHUNK), jnp.float32),
+            pltpu.SemaphoreType.DMA((4, kv_local, 2)),
             pltpu.SemaphoreType.DMA((ctx_size, 2, 4)),
             pltpu.SemaphoreType.DMA((ctx_size, 2, kv_local)),
             pltpu.SemaphoreType.DMA((tp_size - 1, per_peer, kv_local)),

time: 32.7 us -> 30.5 us (0.933)
  Pallas kernels: 31.9 us -> 29.7 us
    pallas_call x1, Pallas kernels: 30.9 us -> 28.7 us  [body(): pl.pallas_call(functools.partial(kernel, dims), out_shape=(pltpu.VMEM((to...]
where the time goes in v4:
time: 30.5 us; the launch traced here: 30.3 us
  Pallas kernels  29.7 us (97%)
  between operations  0.64 us (2%)
    pallas_call x1, Pallas kernels, body(): pl.pallas_call(functools.partial(kernel, dims), out_shape=(pltpu.VMEM((to...  28.7 us
    pallas_call x1, Pallas kernels, body(): pl.pallas_call(copy_out, out_shape=(jax.ShapeDtypeStruct(attended.shape,...  0.99 us

profile of v4, /device:TPU:0, one launch (start us, length us, event | category | flops | bytes accessed | tf_op | source)
XLA Modules:
  0.0 30.3 jit_solution(9699756975303626544)
XLA Ops:
  0.6 28.7 %gather_attend.1 = (bf16[128,4096]{1,0:T(8,128)(2,1)S(1)}, f32[16,256]{1,0:T(8,128)S(1)}) custom-call(bf16[256,2048]{1,0:T(8,128)(2,1)} %queries.1, bf16[256,256]{1,0:T(8,128)(2,1)} %keys.1, bf16[256,256]{1,0:T(8,128)(2,1)} %values.1, s32[1,16]{1,0:T(1,128)} %bitcast.1, s32[16,12]{1,0:T(8,128)} %live_blocks.1), custom_call_target="tpu_custom_call" | custom-call | tf_op jit(solution)/shard_map/gather_attend/pallas_call | solution.py:399
  29.3 1.0 %copy_out.1 = (bf16[128,4096]{1,0:T(8,128)(2,1)}, f32[16,256]{1,0:T(8,128)}) custom-call(bf16[128,4096]{1,0:T(8,128)(2,1)S(1)} %get-tuple-element.4.attended, f32[16,256]{1,0:T(8,128)S(1)} %get-tuple-element.5.log_norm), custom_call_target="tpu_custom_call" | custom-call | tf_op jit(solution)/shard_map/copy_out/pallas_call | solution.py:428

commit v5 on v4

--- a/solution.py
+++ b/solution.py
@@ -44,6 +44,7 @@
     limits,
     scores,
     load_sem,
+    answer,
     send_sem,
     recv_sem,
     swap_send,
@@ -79,7 +80,9 @@
         (b > 0, me - 1),
         (b < minor - 1, me + 1),
     )
-    for there, who in sides:
+    lower, upper = (0, 2), (1, 3)
+    for side in upper:
+        there, who = sides[side]
 
         @pl.when(there)
         def _(who=who):
@@ -91,9 +94,17 @@
     for load in loads + [load_queries] + tables:
         load.start()
     expected = jnp.int32(tp_size - 1)
-    for there, _ in sides:
-        expected = expected + there.astype(jnp.int32)
+    for side in lower:
+        expected = expected + sides[side][0].astype(jnp.int32)
     pl.semaphore_wait(barrier, expected)
+    for side in lower:
+        there, who = sides[side]
+
+        @pl.when(there)
+        def _(who=who, side=side):
+            pl.semaphore_signal(
+                answer.at[side // 2], inc=1, device_id={"ctx": who}, device_id_type=MESH
+            )
 
     def onward(part, i, j):
         column_first = j == b
@@ -107,10 +118,11 @@
             (j <= b) & (b < minor - 1) & across,
         )
 
-    def send_on(slot, part, h, i, j):
-        for side, wanted in enumerate(onward(part, i, j)):
-
-            @pl.when(wanted)
+    def send_on(slot, part, h, i, j, to=range(4)):
+        wanted = onward(part, i, j)
+        for side in to:
+
+            @pl.when(wanted[side])
             def _(side=side):
                 pltpu.make_async_remote_copy(
                     src_ref=held.at[slot, h, :, spans[part]],
@@ -120,6 +132,22 @@
                     device_id={"ctx": sides[side][1]},
                     device_id_type=MESH,
                 ).start()
+
+    def send_own(part, h, to):
+        wanted = onward(part, a, b)
+        for side in to:
+
+            @pl.when(wanted[side])
+            def _(side=side):
+                for kind, source in enumerate((keys, values)):
+                    pltpu.make_async_remote_copy(
+                        src_ref=source.at[spans[part], pl.ds(h * HEAD_SIZE, HEAD_SIZE)],
+                        dst_ref=held.at[me, h, kind, spans[part]],
+                        send_sem=send_sem.at[me, part, side],
+                        recv_sem=recv_sem.at[me, part, h],
+                        device_id={"ctx": sides[side][1]},
+                        device_id_type=MESH,
+                    ).start()
 
     def settle(slot, i, j):
         for part in range(parts):
@@ -148,6 +176,8 @@
     def attend(slots, h, first, after=None):
         keys_here = [held[slot, h, 0] for slot in slots]
         turned_values = jnp.concatenate([jnp.transpose(held[slot, h, 1]) for slot in slots], axis=1)
+        ones = jnp.ones((16, turned_values.shape[1]), turned_values.dtype)
+        turned_values = jnp.concatenate([turned_values, ones], axis=0)
         turned = (mine + 1) * per_peer
         units = [
             (q if first else (turned + q) % blocks_here, q, start)
@@ -193,14 +223,13 @@
                 start_at = n * rows + kb * BLOCK_TOKENS
                 for at in range(start_at, start_at + BLOCK_TOKENS, STRIP):
                     w = jnp.exp2(scores[u % SLOTS, pl.ds(at, STRIP), :] * scale - floor)
-                    added = w if added is None else added + w
                     low.append(w.astype(jnp.bfloat16))
-            added = jnp.sum(added, axis=0, keepdims=True)
             product = jnp.dot(
                 turned_values,
                 jnp.concatenate(low, axis=0),
                 preferred_element_type=jnp.float32,
             )
+            added, product = product[HEAD_SIZE : HEAD_SIZE + 1], product[:HEAD_SIZE]
             if first:
                 weight_sum[query_block, h, :, lanes] = added
                 total[query_block, h, :, lanes] = product
@@ -259,11 +288,22 @@
         if turn < tp_size:
             swap(turn, k, h).start()
 
+    for part in range(parts):
+        send_own(part, 0, lower)
     for load in loads:
         load.wait()
+    for h in range(1, kv_local):
+        for part in range(parts):
+            send_on(me, part, h, a, b, lower)
+    for side in upper:
+
+        @pl.when(sides[side][0])
+        def _(side=side):
+            pl.semaphore_wait(answer.at[side // 2], 1)
+
     for h in range(kv_local):
         for part in range(parts):
-            send_on(me, part, h, a, b)
+            send_on(me, part, h, a, b, upper)
     for load in [load_queries] + tables:
         load.wait()
 
@@ -417,6 +457,7 @@
             pltpu.SMEM((ctx_size, blocks_here, blocks_here), jnp.float32),
             pltpu.VMEM((SLOTS, 2 * tok_rows, CHUNK), jnp.float32),
             pltpu.SemaphoreType.DMA((4, kv_local, 2)),
+            pltpu.SemaphoreType.REGULAR((2,)),
             pltpu.SemaphoreType.DMA((ctx_size, 2, 4)),
             pltpu.SemaphoreType.DMA((ctx_size, 2, kv_local)),
             pltpu.SemaphoreType.DMA((tp_size - 1, per_peer, kv_local)),

time: 30.5 us -> 29.2 us (0.957)
  Pallas kernels: 29.7 us -> 28.4 us
    pallas_call x1, Pallas kernels: 28.7 us -> 27.4 us  [body(): pl.pallas_call(functools.partial(kernel, dims), out_shape=(pltpu.VMEM((to...]
where the time goes in v5:
time: 29.2 us; the launch traced here: 29 us
  Pallas kernels  28.4 us (97%)
  between operations  0.64 us (2%)
    pallas_call x1, Pallas kernels, body(): pl.pallas_call(functools.partial(kernel, dims), out_shape=(pltpu.VMEM((to...  27.4 us
    pallas_call x1, Pallas kernels, body(): pl.pallas_call(copy_out, out_shape=(jax.ShapeDtypeStruct(attended.shape,...  0.99 us

profile of v5, /device:TPU:0, one launch (start us, length us, event | category | flops | bytes accessed | tf_op | source)
XLA Modules:
  0.0 29.0 jit_solution(10052007159626599598)
XLA Ops:
  0.6 27.4 %gather_attend.1 = (bf16[128,4096]{1,0:T(8,128)(2,1)S(1)}, f32[16,256]{1,0:T(8,128)S(1)}) custom-call(bf16[256,2048]{1,0:T(8,128)(2,1)} %queries.1, bf16[256,256]{1,0:T(8,128)(2,1)} %keys.1, bf16[256,256]{1,0:T(8,128)(2,1)} %values.1, s32[1,16]{1,0:T(1,128)} %bitcast.1, s32[16,12]{1,0:T(8,128)} %live_blocks.1), custom_call_target="tpu_custom_call" | custom-call | tf_op jit(solution)/shard_map/gather_attend/pallas_call | solution.py:439
  28.0 1.0 %copy_out.1 = (bf16[128,4096]{1,0:T(8,128)(2,1)}, f32[16,256]{1,0:T(8,128)}) custom-call(bf16[128,4096]{1,0:T(8,128)(2,1)S(1)} %get-tuple-element.4.attended, f32[16,256]{1,0:T(8,128)S(1)} %get-tuple-element.5.log_norm), custom_call_target="tpu_custom_call" | custom-call | tf_op jit(solution)/shard_map/copy_out/pallas_call | solution.py:469

commit v6 on v5

--- a/solution.py
+++ b/solution.py
@@ -13,6 +13,7 @@
 CHUNK = 256
 STRIP = 16
 SLOTS = 4
+VMEM_LIMIT = 60 << 20
 FAR = 1e30
 HUGE = 3e38
 MESH = pl.DeviceIdType.MESH
@@ -60,6 +61,11 @@
     me = lax.axis_index("ctx")
     mine = lax.axis_index("tp")
     a, b = me // minor, me % minor
+    per_peer = blocks_here // tp_size
+
+    def real(q):
+        return ((mine + 1) * per_peer + q) % blocks_here
+
 
     tables = [
         pltpu.make_async_copy(block_order, order, load_sem.at[0, 0, 0]),
@@ -91,7 +97,7 @@
     for turn in range(1, tp_size):
         peer = (mine + turn) % tp_size
         pl.semaphore_signal(barrier, inc=1, device_id={"tp": peer}, device_id_type=MESH)
-    for load in loads + [load_queries] + tables:
+    for load in loads:
         load.start()
     expected = jnp.int32(tp_size - 1)
     for side in lower:
@@ -162,15 +168,15 @@
                     ).wait()
 
     def find_limits(slot, carry):
-        for query_block in range(blocks_here):
-            my_seq = order[0, me * blocks_here + query_block]
+        for q in range(blocks_here):
+            my_seq = order[0, me * blocks_here + real(q)]
             found = [jnp.bool_(False)] * blocks_here
             names = [order[0, slot * blocks_here + kb] for kb in range(blocks_here)]
             for entry in range(slots_live):
                 listed = live[my_seq, entry]
                 found = [f | (listed == name) for f, name in zip(found, names)]
             for kb in range(blocks_here):
-                limits[slot, query_block, kb] = jnp.where(found[kb], HUGE, -FAR)
+                limits[slot, q, kb] = jnp.where(found[kb], HUGE, -FAR)
         return carry
 
     def attend(slots, h, first, after=None):
@@ -178,26 +184,22 @@
         turned_values = jnp.concatenate([jnp.transpose(held[slot, h, 1]) for slot in slots], axis=1)
         ones = jnp.ones((16, turned_values.shape[1]), turned_values.dtype)
         turned_values = jnp.concatenate([turned_values, ones], axis=0)
-        turned = (mine + 1) * per_peer
-        units = [
-            (q if first else (turned + q) % blocks_here, q, start)
-            for q in range(blocks_here)
-            for start in range(0, width, CHUNK)
-        ]
+        units = [(q, start) for q in range(blocks_here) for start in range(0, width, CHUNK)]
         blocks = [(n, slot, kb) for n, slot in enumerate(slots) for kb in range(blocks_here)]
 
         def score(u):
-            query_block, q, start = units[u]
-            turned_here = turned_queries[query_block, h, :, pl.ds(start, CHUNK)]
+            q, start = units[u]
+            turned_here = turned_queries[q, h, :, pl.ds(start, CHUNK)]
             parts = [
                 jnp.dot(k, turned_here, preferred_element_type=jnp.float32) for k in keys_here
             ]
             tops = []
             for n, slot, kb in blocks:
                 block = parts[n][kb * BLOCK_TOKENS : (kb + 1) * BLOCK_TOKENS]
-                if first and kb == q:
+                if first:
                     key_at = lax.broadcasted_iota(jnp.int32, block.shape, 0)
                     row_at = lax.broadcasted_iota(jnp.int32, block.shape, 1) % BLOCK_TOKENS
+                    row_at = row_at + (real(q) != kb).astype(jnp.int32) * BLOCK_TOKENS
                     block = jnp.where(key_at <= row_at, block, -FAR)
                 at = n * rows + kb * BLOCK_TOKENS
                 scores[u % SLOTS, pl.ds(at, BLOCK_TOKENS), :] = block
@@ -205,21 +207,21 @@
             return tops
 
         def absorb(u, tops):
-            query_block, q, start = units[u]
+            q, start = units[u]
             lanes = pl.ds(start, CHUNK)
             new_peak = None
             for (n, slot, kb), top in zip(blocks, tops):
-                top = jnp.minimum(top, limits[slot, query_block, kb])
+                top = jnp.minimum(top, limits[slot, q, kb])
                 new_peak = top if new_peak is None else jnp.maximum(new_peak, top)
             if not first:
-                old_peak = peak[query_block, h, :, lanes]
+                old_peak = peak[q, h, :, lanes]
                 new_peak = jnp.maximum(new_peak, old_peak)
-            peak[query_block, h, :, lanes] = new_peak
+            peak[q, h, :, lanes] = new_peak
             level = new_peak * scale
             added = None
             low = []
             for n, slot, kb in blocks:
-                floor = jnp.maximum(level, -limits[slot, query_block, kb])
+                floor = jnp.maximum(level, -limits[slot, q, kb])
                 start_at = n * rows + kb * BLOCK_TOKENS
                 for at in range(start_at, start_at + BLOCK_TOKENS, STRIP):
                     w = jnp.exp2(scores[u % SLOTS, pl.ds(at, STRIP), :] * scale - floor)
@@ -231,14 +233,14 @@
             )
             added, product = product[HEAD_SIZE : HEAD_SIZE + 1], product[:HEAD_SIZE]
             if first:
-                weight_sum[query_block, h, :, lanes] = added
-                total[query_block, h, :, lanes] = product
+                weight_sum[q, h, :, lanes] = added
+                total[q, h, :, lanes] = product
             else:
                 fade = jnp.exp2((old_peak - new_peak) * scale)
-                weight_sum[query_block, h, :, lanes] = (
-                    weight_sum[query_block, h, :, lanes] * fade + added
+                weight_sum[q, h, :, lanes] = (
+                    weight_sum[q, h, :, lanes] * fade + added
                 )
-                total[query_block, h, :, lanes] = total[query_block, h, :, lanes] * fade + product
+                total[q, h, :, lanes] = total[q, h, :, lanes] * fade + product
 
         waiting = [score(u) for u in range(SLOTS - 1)]
         for u in range(len(units)):
@@ -246,9 +248,8 @@
                 waiting.append(score(u + SLOTS - 1))
             absorb(u, waiting[u])
             if after is not None and (u + 1) % (len(units) // blocks_here) == 0:
-                after(units[u][1])
-
-    per_peer = blocks_here // tp_size
+                after(units[u][0])
+
     wide = kv_local * width
 
     def swap(turn, k, h):
@@ -256,7 +257,7 @@
         source = pl.ds(pl.multiple_of(h * width, HEAD_SIZE), width)
         target = pl.ds(pl.multiple_of(mine * wide + h * width, HEAD_SIZE), width)
         return pltpu.make_async_remote_copy(
-            src_ref=leaving.at[peer * per_peer + k, :, source],
+            src_ref=leaving.at[(turn - 1) * per_peer + k, :, source],
             dst_ref=attended.at[pl.ds(k * BLOCK_TOKENS, BLOCK_TOKENS), target],
             send_sem=swap_send.at[turn - 1, k, h],
             recv_sem=swap_recv.at[turn - 1, k, h],
@@ -266,23 +267,21 @@
 
     def finish(h, q):
         turn, k = 1 + q // per_peer, q % per_peer
-        peer = (mine + turn) % tp_size
-        query_block = peer * per_peer + k
-        at = pl.ds(pl.multiple_of(query_block * BLOCK_TOKENS, BLOCK_TOKENS), BLOCK_TOKENS)
+        at = pl.ds(pl.multiple_of(real(q) * BLOCK_TOKENS, BLOCK_TOKENS), BLOCK_TOKENS)
         norms = []
         for g in range(groups):
             head = h * groups + g
             lanes = pl.ds(g * BLOCK_TOKENS, BLOCK_TOKENS)
-            bottom = weight_sum[query_block, h, :, lanes]
-            normed = total[query_block, h, :, lanes] * (1.0 / bottom)
+            bottom = weight_sum[q, h, :, lanes]
+            normed = total[q, h, :, lanes] * (1.0 / bottom)
             tile = jnp.transpose(normed.astype(jnp.bfloat16))
             if turn < tp_size:
                 to = pl.multiple_of(head * HEAD_SIZE, HEAD_SIZE)
-                leaving[query_block, :, pl.ds(to, HEAD_SIZE)] = tile
+                leaving[q, :, pl.ds(to, HEAD_SIZE)] = tile
             else:
                 to = pl.multiple_of(mine * wide + head * HEAD_SIZE, HEAD_SIZE)
                 attended[pl.ds(k * BLOCK_TOKENS, BLOCK_TOKENS), pl.ds(to, HEAD_SIZE)] = tile
-            norms.append(peak[query_block, h, :, lanes] * factor + jnp.log(bottom))
+            norms.append(peak[q, h, :, lanes] * factor + jnp.log(bottom))
         heads = pl.ds(pl.multiple_of(h * groups, groups), groups)
         log_norm[heads, at] = jnp.concatenate(norms, axis=0)
         if turn < tp_size:
@@ -290,6 +289,8 @@
 
     for part in range(parts):
         send_own(part, 0, lower)
+    for load in [load_queries] + tables:
+        load.start()
     for load in loads:
         load.wait()
     for h in range(1, kv_local):
@@ -307,13 +308,13 @@
     for load in [load_queries] + tables:
         load.wait()
 
-    def turn_block(query_block, carry):
-        at = pl.ds(pl.multiple_of(query_block * BLOCK_TOKENS, BLOCK_TOKENS), BLOCK_TOKENS)
+    def turn_block(q, carry):
+        at = pl.ds(pl.multiple_of(real(q) * BLOCK_TOKENS, BLOCK_TOKENS), BLOCK_TOKENS)
         for h in range(kv_local):
             for g in range(groups):
                 head = h * groups + g
-                turned_queries[query_block, h, :, pl.ds(g * BLOCK_TOKENS, BLOCK_TOKENS)] = (
-                    jnp.transpose(raw_queries[at, pl.ds(head * HEAD_SIZE, HEAD_SIZE)])
+                turned_queries[q, h, :, pl.ds(g * BLOCK_TOKENS, BLOCK_TOKENS)] = jnp.transpose(
+                    raw_queries[at, pl.ds(head * HEAD_SIZE, HEAD_SIZE)]
                 )
         return carry
 
@@ -463,7 +464,9 @@
             pltpu.SemaphoreType.DMA((tp_size - 1, per_peer, kv_local)),
             pltpu.SemaphoreType.DMA((tp_size - 1, per_peer, kv_local)),
         ],
-        compiler_params=pltpu.CompilerParams(collective_id=0, has_side_effects=True),
+        compiler_params=pltpu.CompilerParams(
+            collective_id=0, has_side_effects=True, vmem_limit_bytes=VMEM_LIMIT
+        ),
         name="gather_attend",
     )(queries, rotated_key_rows, ordered_value_rows, block_order.reshape(1, -1), live_blocks)
     return pl.pallas_call(

time: 29.2 us -> 29.2 us (level)
  no operation moved by 1% of the time
where the time goes in v6:
time: 29.2 us; the launch traced here: 29 us
  Pallas kernels  28.4 us (97%)
  between operations  0.64 us (2%)
    pallas_call x1, Pallas kernels, body(): pl.pallas_call(functools.partial(kernel, dims), out_shape=(pltpu.VMEM((to...  27.4 us
    pallas_call x1, Pallas kernels, body(): pl.pallas_call(copy_out, out_shape=(jax.ShapeDtypeStruct(attended.shape,...  0.99 us

profile of v6, /device:TPU:0, one launch (start us, length us, event | category | flops | bytes accessed | tf_op | source)
XLA Modules:
  0.0 29.0 jit_solution(7909592437340010126)
XLA Ops:
  0.6 27.4 %gather_attend.1 = (bf16[128,4096]{1,0:T(8,128)(2,1)S(1)}, f32[16,256]{1,0:T(8,128)S(1)}) custom-call(bf16[256,2048]{1,0:T(8,128)(2,1)} %queries.1, bf16[256,256]{1,0:T(8,128)(2,1)} %keys.1, bf16[256,256]{1,0:T(8,128)(2,1)} %values.1, s32[1,16]{1,0:T(1,128)} %bitcast.1, s32[16,12]{1,0:T(8,128)} %live_blocks.1), custom_call_target="tpu_custom_call" | custom-call | tf_op jit(solution)/shard_map/gather_attend/pallas_call | solution.py:440
  28.0 1.0 %copy_out.1 = (bf16[128,4096]{1,0:T(8,128)(2,1)}, f32[16,256]{1,0:T(8,128)}) custom-call(bf16[128,4096]{1,0:T(8,128)(2,1)S(1)} %get-tuple-element.4.attended, f32[16,256]{1,0:T(8,128)S(1)} %get-tuple-element.5.log_norm), custom_call_target="tpu_custom_call" | custom-call | tf_op jit(solution)/shard_map/copy_out/pallas_call | solution.py:472

commit v7 on v6

--- a/solution.py
+++ b/solution.py
@@ -11,7 +11,7 @@
 HEAD_SIZE = 128
 BLOCK_TOKENS = 128
 CHUNK = 256
-STRIP = 16
+STRIP = 32
 SLOTS = 4
 VMEM_LIMIT = 60 << 20
 FAR = 1e30

time: 29.2 us -> 29.2 us (level)
  no operation moved by 1% of the time
where the time goes in v7:
time: 29.2 us; the launch traced here: 29 us
  Pallas kernels  28.4 us (97%)
  between operations  0.64 us (2%)
    pallas_call x1, Pallas kernels, body(): pl.pallas_call(functools.partial(kernel, dims), out_shape=(pltpu.VMEM((to...  27.4 us
    pallas_call x1, Pallas kernels, body(): pl.pallas_call(copy_out, out_shape=(jax.ShapeDtypeStruct(attended.shape,...  0.99 us

profile of v7, /device:TPU:0, one launch (start us, length us, event | category | flops | bytes accessed | tf_op | source)
XLA Modules:
  0.0 29.0 jit_solution(7909592437340010126)
XLA Ops:
  0.6 27.4 %gather_attend.1 = (bf16[128,4096]{1,0:T(8,128)(2,1)S(1)}, f32[16,256]{1,0:T(8,128)S(1)}) custom-call(bf16[256,2048]{1,0:T(8,128)(2,1)} %queries.1, bf16[256,256]{1,0:T(8,128)(2,1)} %keys.1, bf16[256,256]{1,0:T(8,128)(2,1)} %values.1, s32[1,16]{1,0:T(1,128)} %bitcast.1, s32[16,12]{1,0:T(8,128)} %live_blocks.1), custom_call_target="tpu_custom_call" | custom-call | tf_op jit(solution)/shard_map/gather_attend/pallas_call | solution.py:440
  28.0 1.0 %copy_out.1 = (bf16[128,4096]{1,0:T(8,128)(2,1)}, f32[16,256]{1,0:T(8,128)}) custom-call(bf16[128,4096]{1,0:T(8,128)(2,1)S(1)} %get-tuple-element.4.attended, f32[16,256]{1,0:T(8,128)S(1)} %get-tuple-element.5.log_norm), custom_call_target="tpu_custom_call" | custom-call | tf_op jit(solution)/shard_map/copy_out/pallas_call | solution.py:472
